TPU v7x, 128 devices: a whole 4x4x4 slice. The times are simulated.
128 devices in a mesh: row: 8 (over y, core), col: 16 (over x, z).
Axes of the slice: x: 4, y: 4, z: 4, core: 2. Of those that a mesh axis runs over, the one named last changes fastest.
Arguments:
- scores: float32 [32, 98304], P(None, ('row', 'col')), may hold values from -60 to 60
- tile_values: bfloat16 [8, 16, 480, 128, 128], P('row', 'col'), may hold values from 0 to 1
- tile_rows: int32 [8, 16, 480], P('row', 'col'), may hold values from 0 to 95, as said below
- tile_cols: int32 [8, 16, 480], P('row', 'col'), may hold values from 0 to 47, as said below
- tile_count: int32 [8, 16], P('row', 'col'), may hold values from 240 to 480, as said below
Outputs:
- solution: float32 [32, 98304], P(None, ('row', 'col'))
- residual: float32 [32, 98304], P(None, ('row', 'col'))
Inputs may be any that keep to these rules, and one draw needn't show every extreme that they name: `tile_rows`: on every device each local row tile is named by exactly 5 of the 480 slots. `tile_cols`: on every device each local column tile is named by exactly 10 of the slots. Only the first tile_count slots of a device are live; some device has all 480 slots live.
All inputs are finite; a program needn't handle non-finite values.
Results may differ from a plain program's by a relative error of at most 0.0031.
Values may be sent and summed in bfloat16 or wider, within the bound.
A program may use at most 128 MiB of HBM per device.

v0:
```python
import jax
import jax.numpy as jnp
from jax import lax
from jax.sharding import PartitionSpec as P

PER_ROW = 5
ITERS = 3


coupling = 0.2


def per_device(scores, tile_values, tile_rows, tile_cols, tile_count):
    tile_blocks = tile_values[0, 0]
    row_tile_ids = tile_rows[0, 0]
    col_tile_ids = tile_cols[0, 0]
    live_count = tile_count[0, 0]
    slot_count = tile_blocks.shape[0]
    tile_size = tile_blocks.shape[1]
    task_count = scores.shape[0]
    piece_len = scores.shape[1]
    row_span = piece_len * lax.axis_size("col")
    col_span = piece_len * lax.axis_size("row")
    row_tiles = row_span // tile_size
    col_tiles = col_span // tile_size
    block_slots = slot_count // PER_ROW
    live_mask = (jnp.arange(slot_count, dtype=jnp.int32) < live_count).astype(jnp.float32)
    row_weight = jnp.sum(tile_blocks, axis=2, dtype=jnp.float32) * live_mask[:, None]
    col_weight = jnp.sum(tile_blocks, axis=1, dtype=jnp.float32) * live_mask[:, None]
    row_degree_part = (
        jnp.zeros((row_tiles, tile_size), jnp.float32)
        .at[row_tile_ids]
        .add(row_weight)
        .reshape(1, row_span)
    )
    col_degree_part = (
        jnp.zeros((col_tiles, tile_size), jnp.float32)
        .at[col_tile_ids]
        .add(col_weight)
        .reshape(1, col_span)
    )

    def to_rows(partial_value):
        return lax.psum_scatter(partial_value, "col", scatter_dimension=1, tiled=True)

    def to_cols(partial_value):
        return lax.psum_scatter(partial_value, "row", scatter_dimension=1, tiled=True)

    degree = 0.5 * (to_rows(row_degree_part) + to_cols(col_degree_part))

    def inner_sums(parts):
        return lax.psum(parts, ("row", "col"))

    solution = jnp.zeros_like(scores)
    residual = scores
    direction = scores
    norm_now = inner_sums(jnp.sum(residual * residual, axis=1))
    for step_index in range(ITERS):
        graph_own_low = direction.astype(jnp.bfloat16)
        graph_col_dir = lax.all_gather(graph_own_low, "row", axis=1, tiled=True)
        graph_row_dir = lax.all_gather(graph_own_low, "col", axis=1, tiled=True)
        col_blocks = graph_col_dir.reshape(task_count, col_tiles, tile_size)
        row_blocks = graph_row_dir.reshape(task_count, row_tiles, tile_size)
        block_count = (live_count + block_slots - 1) // block_slots

        def one_block(block_index, totals):
            forward_sum, backward_sum = totals
            first_slot = block_index * block_slots
            tiles_here = lax.dynamic_slice_in_dim(tile_blocks, first_slot, block_slots, 0)
            rows_here = lax.dynamic_slice_in_dim(row_tile_ids, first_slot, block_slots, 0)
            cols_here = lax.dynamic_slice_in_dim(col_tile_ids, first_slot, block_slots, 0)
            live_here = (first_slot + jnp.arange(block_slots, dtype=jnp.int32) < live_count).astype(
                jnp.float32
            )
            col_pieces = jnp.take(col_blocks, cols_here, axis=1)
            row_pieces = jnp.take(row_blocks, rows_here, axis=1)
            forward = (
                jnp.einsum(
                    "ksd,sod->kso", col_pieces, tiles_here, preferred_element_type=jnp.float32
                )
                * live_here[None, :, None]
            )
            backward = (
                jnp.einsum(
                    "kso,sod->ksd", row_pieces, tiles_here, preferred_element_type=jnp.float32
                )
                * live_here[None, :, None]
            )
            return (
                forward_sum.at[:, rows_here, :].add(forward),
                backward_sum.at[:, cols_here, :].add(backward),
            )

        empty_sums = (
            jnp.zeros((task_count, row_tiles, tile_size), jnp.float32),
            jnp.zeros((task_count, col_tiles, tile_size), jnp.float32),
        )
        forward_sum, backward_sum = lax.fori_loop(0, block_count, one_block, empty_sums)
        forward_part = forward_sum.reshape(task_count, row_span)
        backward_part = backward_sum.reshape(task_count, col_span)
        image_field = direction + coupling * (
            degree * direction - 0.5 * (to_rows(forward_part) + to_cols(backward_part))
        )
        curvature = inner_sums(jnp.sum(direction * image_field, axis=1))
        step_size = norm_now / curvature
        solution = solution + step_size[:, None] * direction
        residual = residual - step_size[:, None] * image_field
        if step_index + 1 < ITERS:
            norm_next = inner_sums(jnp.sum(residual * residual, axis=1))
            direction = residual + (norm_next / norm_now)[:, None] * direction
            norm_now = norm_next
    return (solution, residual)


def solution(mesh):
    return jax.shard_map(
        per_device,
        mesh=mesh,
        in_specs=(
            P(None, ("row", "col")),
            P("row", "col", None, None, None),
            P("row", "col", None),
            P("row", "col", None),
            P("row", "col"),
        ),
        out_specs=(P(None, ("row", "col")), P(None, ("row", "col"))),
        check_vma=False,
    )
```

profile of v0, /device:TPU:0, one launch (start us, length us, event | category | flops | bytes accessed | tf_op | source)
XLA Modules:
  0.0 1217.4 jit_solution(540083142210740069)
XLA Ops:
  7.9 9.8 convert_reduce_fusion
  30.8 26.8 %all_gather.19 = bf16[32,12288]{1,0:T(8,128)(2,1)S(1)} all-gather(bf16[32,768]{1,0:T(8,128)(2,1)S(1)} %convert_element_type.43), channel_id=1, replica_groups=mesh['row'=8,'col'=16] {'col'}, dimensions={1}, use_global_device_ids=true | all-gather | bytes 835584 | tf_op jit(solution)/shard_map/all_gather | solution.py:61
  57.6 13.0 %all_gather.18 = bf16[32,6144]{1,0:T(8,128)(2,1)S(1)} all-gather(bf16[32,768]{1,0:T(8,128)(2,1)S(1)} %convert_element_type.43), channel_id=1, replica_groups=mesh['row'=8,'col'=16] {'row'}, dimensions={1}, use_global_device_ids=true | all-gather | bytes 442368 | tf_op jit(solution)/shard_map/all_gather | solution.py:60
  73.2 137.2 %while.36 = (s32[]{:T(128)}, f32[32,96,128]{2,0,1:T(8,128)}, f32[32,48,128]{2,0,1:T(8,128)S(1)}, s32[]{:T(128)}, s32[480]{0:T(512)}, /*index=5*/bf16[480,128,128...) while((s32[]{:T(128)}, f32[32,96,128]{2,0,1:T(8,128)}, ...), condition=%wide.region_11.14_spmd, body=%wide.region_8.13_spmd.sunk | while | flops 203689376 | bytes 23607144 | solution.py:98
  79.5 11.9 scatter_fusion
  107.1 11.9 scatter_fusion
  123.7 4.4 scatter_fusion.1
  134.7 11.8 scatter_fusion
  151.2 4.4 scatter_fusion.1
  162.1 11.8 scatter_fusion
  178.6 4.4 scatter_fusion.1
  189.4 11.8 scatter_fusion
  205.9 4.4 scatter_fusion.1
  215.8 25.9 %reduce-scatter.15.cloned.1.call-done = f32[32,768]{1,0:T(8,128)} async-done(((f32[32,6144]{1,0:T(8,128)}), f32[32,768]{1,0:T(8,128)}) %reduce-scatter.15.cloned.1.call-update) | async-done | bytes 98320 | tf_op jit(solution)/shard_map/reduce_scatter | solution.py:47
  241.7 76.5 %reduce-scatter.13.cloned.1.call-done = f32[32,768]{1,0:T(8,128)} async-done(((f32[32,12288]{1,0:T(8,128)}), f32[32,768]{1,0:T(8,128)}) %reduce-scatter.13.cloned.1.call-update) | async-done | bytes 98320 | tf_op jit(solution)/shard_map/reduce_scatter | solution.py:44
  319.2 64.8 %all-reduce = (f32[32]{0:T(128)S(1)}, f32[32]{0:T(128)S(1)}) all-reduce(f32[32]{0:T(128)S(1)} %get-tuple-element.255, f32[32]{0:T(128)S(1)} %get-tuple-element.254), channel_id=1, replica_groups=mesh['row'=8,'col'=16] {'row','col'}, use_global_device_ids=true, to_apply=%region_1.0 | all-reduce | flops 64 | bytes 512 | tf_op jit(solution)/shard_map/psum | solution.py:52
  385.2 62.0 %psum.44 = f32[32]{0:T(128)S(1)} all-reduce(f32[32]{0:T(128)S(1)} %get-tuple-element.334), channel_id=1, replica_groups=mesh['row'=8,'col'=16] {'row','col'}, use_global_device_ids=true, to_apply=%region_17.20 | all-reduce | flops 32 | bytes 256 | tf_op jit(solution)/shard_map/psum | solution.py:52
  448.0 24.2 %all_gather.21 = bf16[32,12288]{1,0:T(8,128)(2,1)S(1)} all-gather(bf16[32,768]{1,0:T(8,128)(2,1)S(1)} %get-tuple-element.332), channel_id=1, replica_groups=mesh['row'=8,'col'=16] {'col'}, dimensions={1}, use_global_device_ids=true | all-gather | bytes 835584 | tf_op jit(solution)/shard_map/all_gather | solution.py:61
  472.1 13.0 %all_gather.20 = bf16[32,6144]{1,0:T(8,128)(2,1)S(1)} all-gather(bf16[32,768]{1,0:T(8,128)(2,1)S(1)} %get-tuple-element.332), channel_id=1, replica_groups=mesh['row'=8,'col'=16] {'row'}, dimensions={1}, use_global_device_ids=true | all-gather | bytes 442368 | tf_op jit(solution)/shard_map/all_gather | solution.py:60
  487.6 136.9 %while.37 = (s32[]{:T(128)}, f32[32,96,128]{2,0,1:T(8,128)}, f32[32,48,128]{2,0,1:T(8,128)S(1)}, s32[]{:T(128)}, s32[480]{0:T(512)}, /*index=5*/bf16[480,128,128...) while((s32[]{:T(128)}, f32[32,96,128]{2,0,1:T(8,128)}, ...), condition=%wide.region_21.24_spmd, body=%wide.region_18.23_spmd.sunk | while | flops 203689376 | bytes 23607556 | solution.py:98
  494.0 11.8 scatter_fusion.2
  521.4 11.8 scatter_fusion.2
  537.9 4.4 scatter_fusion.3
  548.8 11.8 scatter_fusion.2
  565.3 4.4 scatter_fusion.3
  576.2 11.8 scatter_fusion.2
  592.7 4.4 scatter_fusion.3
  603.6 11.8 scatter_fusion.2
  620.1 4.4 scatter_fusion.3
  627.6 26.6 %reduce-scatter.19.cloned.1.call-done = f32[32,768]{1,0:T(8,128)} async-done(((f32[32,6144]{1,0:T(8,128)}), f32[32,768]{1,0:T(8,128)}) %reduce-scatter.19.cloned.1.call-update) | async-done | bytes 98320 | tf_op jit(solution)/shard_map/reduce_scatter | solution.py:47
  654.3 76.5 %reduce-scatter.17.cloned.1.call-done = f32[32,768]{1,0:T(8,128)} async-done(((f32[32,12288]{1,0:T(8,128)}), f32[32,768]{1,0:T(8,128)}) %reduce-scatter.17.cloned.1.call-update) | async-done | bytes 98320 | tf_op jit(solution)/shard_map/reduce_scatter | solution.py:44
  731.8 64.7 %psum.45 = f32[32]{0:T(128)S(1)} all-reduce(f32[32]{0:T(128)S(1)} %multiply_reduce_fusion.2), channel_id=1, replica_groups=mesh['row'=8,'col'=16] {'row','col'}, use_global_device_ids=true, to_apply=%region_25.28 | all-reduce | flops 32 | bytes 256 | tf_op jit(solution)/shard_map/psum | solution.py:52
  797.7 62.0 %psum.46 = f32[32]{0:T(128)S(1)} all-reduce(f32[32]{0:T(128)S(1)} %get-tuple-element.330), channel_id=1, replica_groups=mesh['row'=8,'col'=16] {'row','col'}, use_global_device_ids=true, to_apply=%region_27.30 | all-reduce | flops 32 | bytes 256 | tf_op jit(solution)/shard_map/psum | solution.py:52
  859.8 24.2 %all_gather.23 = bf16[32,12288]{1,0:T(8,128)(2,1)S(1)} all-gather(bf16[32,768]{1,0:T(8,128)(2,1)S(1)} %fusion.69), channel_id=1, replica_groups=mesh['row'=8,'col'=16] {'col'}, dimensions={1}, use_global_device_ids=true | all-gather | bytes 835584 | tf_op jit(solution)/shard_map/all_gather | solution.py:61
  883.9 13.2 %all_gather.22 = bf16[32,6144]{1,0:T(8,128)(2,1)S(1)} all-gather(bf16[32,768]{1,0:T(8,128)(2,1)S(1)} %fusion.69), channel_id=1, replica_groups=mesh['row'=8,'col'=16] {'row'}, dimensions={1}, use_global_device_ids=true | all-gather | bytes 442368 | tf_op jit(solution)/shard_map/all_gather | solution.py:60
  899.7 136.9 %while.38 = (s32[]{:T(128)}, f32[32,96,128]{2,0,1:T(8,128)}, f32[32,48,128]{2,0,1:T(8,128)S(1)}, s32[]{:T(128)}, s32[480]{0:T(512)}, /*index=5*/bf16[480,128,128...) while((s32[]{:T(128)}, f32[32,96,128]{2,0,1:T(8,128)}, ...), condition=%wide.region_31.34_spmd, body=%wide.region_28.33_spmd.sunk | while | flops 203689376 | bytes 23607556 | solution.py:98
  906.1 11.8 scatter_fusion.4
  933.5 11.8 scatter_fusion.4
  950.0 4.4 scatter_fusion.5
  960.8 11.8 scatter_fusion.4
  977.4 4.4 scatter_fusion.5
  988.2 11.8 scatter_fusion.4
  1004.8 4.4 scatter_fusion.5
  1015.6 11.8 scatter_fusion.4
  1032.2 4.4 scatter_fusion.5
  1039.7 26.7 %reduce-scatter.23.cloned.1.call-done = f32[32,768]{1,0:T(8,128)} async-done(((f32[32,6144]{1,0:T(8,128)}), f32[32,768]{1,0:T(8,128)}) %reduce-scatter.23.cloned.1.call-update) | async-done | bytes 98320 | tf_op jit(solution)/shard_map/reduce_scatter | solution.py:47
  1066.3 76.6 %reduce-scatter.21.cloned.1.call-done = f32[32,768]{1,0:T(8,128)} async-done(((f32[32,12288]{1,0:T(8,128)}), f32[32,768]{1,0:T(8,128)}) %reduce-scatter.21.cloned.1.call-update) | async-done | bytes 98320 | tf_op jit(solution)/shard_map/reduce_scatter | solution.py:44
  1144.1 64.7 %psum.47 = f32[32]{0:T(128)S(1)} all-reduce(f32[32]{0:T(128)S(1)} %multiply_reduce_fusion), channel_id=1, replica_groups=mesh['row'=8,'col'=16] {'row','col'}, use_global_device_ids=true, to_apply=%region_35.38 | all-reduce | flops 32 | bytes 256 | tf_op jit(solution)/shard_map/psum | solution.py:52
  (247 shorter events, 220.0 us)
Async XLA Ops:
  7.2 206.3 %reduce-scatter.27.cloned.1.call-start = ((), (), s32[]{:S(2)}) async-start(), calls=%async_computation.15 | async-start | bytes 3538944
  22.9 191.6 %reduce-scatter.25.cloned.1.call-start = ((), (), s32[]{:S(2)}) async-start(), calls=%async_computation.14 | async-start | bytes 6684672
  29.9 0.9 copy-start.5
  30.0 211.7 %reduce-scatter.15.cloned.1.call-start = ((), (), s32[]{:S(2)}) async-start(), calls=%async_computation.9 | async-start | bytes 884736 | tf_op jit(solution)/shard_map/reduce_scatter | solution.py:47
  210.4 1.7 copy-start.1
  211.4 106.8 %reduce-scatter.13.cloned.1.call-start = ((), (), s32[]{:S(2)}) async-start(), calls=%async_computation.8 | async-start | bytes 1671168 | tf_op jit(solution)/shard_map/reduce_scatter | solution.py:44
  213.3 104.8 %copy-start.6 = (f32[32,768]{1,0:T(8,128)S(1)}, f32[32,768]{1,0:T(8,128)}, u32[]{:S(2)}) copy-start(f32[32,768]{1,0:T(8,128)} %param.15) | copy-start | bytes 294916
  213.4 440.9 %reduce-scatter.19.cloned.1.call-start = ((), (), s32[]{:S(2)}) async-start(), calls=%async_computation.11 | async-start | bytes 884736 | tf_op jit(solution)/shard_map/reduce_scatter | solution.py:47
  384.1 102.0 %copy-start.16 = (f32[32]{0:T(128)}, f32[32]{0:T(128)S(1)}, u32[]{:S(2)}) copy-start(f32[32]{0:T(128)S(1)} %div.22) | copy-start | bytes 388
  385.2 100.9 %copy-start.10 = (f32[32,768]{1,0:T(8,128)}, f32[32,768]{1,0:T(8,128)S(1)}, u32[]{:S(2)}) copy-start(f32[32,768]{1,0:T(8,128)S(1)} %get-tuple-element.335) | copy-start | bytes 294916
  447.2 38.9 %copy-start.20 = (f32[32]{0:T(128)}, f32[32]{0:T(128)S(1)}, u32[]{:S(2)}) copy-start(f32[32]{0:T(128)S(1)} %psum.44) | copy-start | bytes 388
  505.8 1.9 copy-start.12
  533.2 1.9 copy-start.12
  560.6 1.9 copy-start.12
  588.0 1.9 copy-start.12
  615.4 1.9 copy-start.12
  624.6 1.7 copy-start.2
  625.6 105.2 %reduce-scatter.17.cloned.1.call-start = ((), (), s32[]{:S(2)}) async-start(), calls=%async_computation.10 | async-start | bytes 1671168 | tf_op jit(solution)/shard_map/reduce_scatter | solution.py:44
  627.5 103.2 %copy-start.3 = (f32[32,768]{1,0:T(8,128)S(1)}, f32[32,768]{1,0:T(8,128)}, u32[]{:S(2)}) copy-start(f32[32,768]{1,0:T(8,128)} %get-tuple-element.333) | copy-start | bytes 294916
  627.5 168.9 %copy-start.21 = (f32[32]{0:T(128)S(1)}, f32[32]{0:T(128)}, u32[]{:S(2)}) copy-start(f32[32]{0:T(128)} %copy-done.20) | copy-start | bytes 388
  627.5 169.0 %copy-start.11 = (f32[32,768]{1,0:T(8,128)S(1)}, f32[32,768]{1,0:T(8,128)}, u32[]{:S(2)}) copy-start(f32[32,768]{1,0:T(8,128)} %copy-done.10) | copy-start | bytes 294916
  627.6 438.7 %reduce-scatter.23.cloned.1.call-start = ((), (), s32[]{:S(2)}) async-start(), calls=%async_computation.13 | async-start | bytes 884736 | tf_op jit(solution)/shard_map/reduce_scatter | solution.py:47
  796.5 101.6 %copy-start.18 = (f32[32]{0:T(128)}, f32[32]{0:T(128)S(1)}, u32[]{:S(2)}) copy-start(f32[32]{0:T(128)S(1)} %div.24) | copy-start | bytes 388
  797.6 100.6 %copy-start.8 = (f32[32,768]{1,0:T(8,128)}, f32[32,768]{1,0:T(8,128)S(1)}, u32[]{:S(2)}) copy-start(f32[32,768]{1,0:T(8,128)S(1)} %get-tuple-element.331) | copy-start | bytes 294916
  859.7 38.6 %copy-start.22 = (f32[32]{0:T(128)}, f32[32]{0:T(128)S(1)}, u32[]{:S(2)}) copy-start(f32[32]{0:T(128)S(1)} %psum.46) | copy-start | bytes 388
  859.7 38.6 %copy-start.14 = (f32[32]{0:T(128)}, f32[32]{0:T(128)S(1)}, u32[]{:S(2)}) copy-start(f32[32]{0:T(128)S(1)} %div.25) | copy-start | bytes 388
  917.9 1.9 copy-start.13
  945.2 1.9 copy-start.13
  972.6 1.9 copy-start.13
  1000.0 1.9 copy-start.13
  1027.4 1.9 copy-start.13
  1036.6 1.7 copy-start
  1037.6 105.3 %reduce-scatter.21.cloned.1.call-start = ((), (), s32[]{:S(2)}) async-start(), calls=%async_computation.12 | async-start | bytes 1671168 | tf_op jit(solution)/shard_map/reduce_scatter | solution.py:44
  1039.6 103.4 %copy-start.4 = (f32[32,768]{1,0:T(8,128)S(1)}, f32[32,768]{1,0:T(8,128)}, u32[]{:S(2)}) copy-start(f32[32,768]{1,0:T(8,128)} %get-tuple-element.333) | copy-start | bytes 294916
  1039.6 103.4 %copy-start.9 = (f32[32,768]{1,0:T(8,128)S(1)}, f32[32,768]{1,0:T(8,128)}, u32[]{:S(2)}) copy-start(f32[32,768]{1,0:T(8,128)} %copy-done.8) | copy-start | bytes 294916
  1039.6 103.4 %copy-start.15 = (f32[32]{0:T(128)S(1)}, f32[32]{0:T(128)}, u32[]{:S(2)}) copy-start(f32[32]{0:T(128)} %copy-done.14) | copy-start | bytes 388
  1039.6 169.2 %copy-start.23 = (f32[32]{0:T(128)S(1)}, f32[32]{0:T(128)}, u32[]{:S(2)}) copy-start(f32[32]{0:T(128)} %copy-done.22) | copy-start | bytes 388
  1039.6 169.2 %copy-start.7 = (f32[32,768]{1,0:T(8,128)S(1)}, f32[32,768]{1,0:T(8,128)}, u32[]{:S(2)}) copy-start(f32[32,768]{1,0:T(8,128)} %param.15) | copy-start | bytes 294916
  1039.6 169.2 %copy-start.17 = (f32[32]{0:T(128)S(1)}, f32[32]{0:T(128)}, u32[]{:S(2)}) copy-start(f32[32]{0:T(128)} %copy-done.16) | copy-start | bytes 388
  1039.6 169.2 %copy-start.19 = (f32[32]{0:T(128)S(1)}, f32[32]{0:T(128)}, u32[]{:S(2)}) copy-start(f32[32]{0:T(128)} %copy-done.18) | copy-start | bytes 388
Sparse Core Ops, SparseCore 0:
  23.1 38.6 reduce-scatter.26
  65.2 80.9 reduce-scatter.24
  211.5 30.1 reduce-scatter.14
  244.8 73.3 reduce-scatter.12
  625.7 28.5 reduce-scatter.18
  657.3 73.3 reduce-scatter.16
  1037.7 28.5 reduce-scatter.22
  1069.5 73.3 reduce-scatter.20
where the time goes:
time: 1230 us; the launch traced here: 1220 us
  blocking collectives  432 us (35%)
  waiting for transfers between devices  309 us (25%)
  other arithmetic  297 us (24%)
  matrix products  98.7 us (8%)
  local copies, waits for them, and re-layouts  64 us (5%)
  between operations  15.1 us (1%)
    psum x5, blocking collectives, inner_sums(): return lax.psum(parts, ('row', 'col'))  318 us
    reduce_scatter x3, waiting for transfers between devices, to_rows(): lax.psum_scatter(partial_value, 'col', scatter_dimension=1, tiled=True)  230 us
    scatter-add x15, other arithmetic, one_block(): forward_sum.at[:, rows_here, :].add(forward)  177 us
    reduce_scatter x3, waiting for transfers between devices, to_cols(): lax.psum_scatter(partial_value, 'row', scatter_dimension=1, tiled=True)  79.2 us
    all_gather x3, blocking collectives, per_device(): graph_row_dir = lax.all_gather(graph_own_low, 'col', axis=1, tiled=True)  75.1 us
    scatter-add x15, other arithmetic, one_block(): backward_sum.at[:, cols_here, :].add(backward)  66.6 us
    dot_general x15, matrix products, one_block(): jnp.einsum('ksd,sod->kso', col_pieces, tiles_here, preferred_element_type...  55.4 us
    dot_general x15, matrix products, one_block(): jnp.einsum('kso,sod->ksd', row_pieces, tiles_here, preferred_element_type...  43.3 us
  transfers between devices with their start and end apart: 8, of which 6 were waited for; matrix products, arithmetic and copies ran while one was open for 13% of the time, Pallas kernels for 0%

commit v1 on v0

v1 whole, which is shorter than its diff:
```python
import functools

import jax
import jax.numpy as jnp
from jax import lax
from jax.experimental import pallas as pl
from jax.experimental.pallas import tpu as pltpu
from jax.sharding import PartitionSpec as P

PER_ROW = 5
ITERS = 3
MESH = pl.DeviceIdType.MESH
SUM_TYPE = jnp.float32

coupling = 0.2


def spread(n):
    fast = 2 if n <= 8 else 4
    return n // fast, fast


def partner(me, k, n):
    slow, fast = spread(n)
    a = lax.rem(me // fast + slow // 2 + k // fast, slow)
    b = lax.rem(lax.rem(me, fast) + fast // 2 + lax.rem(k, fast), fast)
    return a * fast + b


def own_turn(n):
    slow, fast = spread(n)
    return (slow - slow // 2) % slow * fast + (fast - fast // 2) % fast


def cg_kernel(
    n_row, n_col, per_col,
    row_table, col_table, scores, tiles_hbm, sol, res,
    tiles, x_col, x_row, f_part, b_part, f_recv, b_recv,
    df_part, db_part, df_recv, db_recv, ones, dir_ref, degree, dots_row, dots_col,
    tile_sem,
    agr_send, agr_recv, agc_send, agc_recv,
    rsf_send, rsf_recv, rsb_send, rsb_recv,
    dgf_send, dgf_recv, dgb_send, dgb_recv,
    d1_send, d1_recv, d2_send, d2_recv,
):
    me_r = lax.axis_index("row")
    me_c = lax.axis_index("col")
    tasks = scores.shape[0]
    own_tiles = scores.shape[1] // 128
    slots = tiles.shape[0]
    col_tiles = b_part.shape[0]
    row_tiles = f_part.shape[0]
    chunk = slots // tile_sem.shape[0]

    def tile_copy(i):
        part = pl.ds(i * chunk, chunk)
        return pltpu.make_async_copy(tiles_hbm.at[part], tiles.at[part], tile_sem.at[i])

    for i in range(tile_sem.shape[0]):
        tile_copy(i).start()

    barrier = pltpu.get_barrier_semaphore()

    def greet(axis, n, own):
        def one(k, carry):
            @pl.when(k != own_turn(n))
            def _():
                j = partner(own, k, n)
                target = (me_r, j) if axis == "col" else (j, me_c)
                pl.semaphore_signal(barrier, inc=1, device_id=target, device_id_type=MESH)
            return carry

        lax.fori_loop(0, n, one, 0)

    greet("col", n_col, me_c)
    greet("row", n_row, me_r)

    x_col[col_tiles] = jnp.zeros((tasks, 128), jnp.bfloat16)
    x_row[row_tiles] = jnp.zeros((tasks, 128), jnp.bfloat16)
    ones[0] = jnp.ones((16, 128), jnp.bfloat16)
    ones[1] = jnp.zeros((16, 128), jnp.bfloat16)
    dir_ref[...] = scores[...]
    res[...] = scores[...]
    sol[...] = jnp.zeros_like(sol)

    pl.semaphore_wait(barrier, n_row + n_col - 2)

    def each_partner(n, own, action):
        def one(k, carry):
            @pl.when(k != own_turn(n))
            def _():
                action(partner(own, k, n))
            return carry

        lax.fori_loop(0, n, one, 0)

    own_col = pl.ds(me_r * own_tiles, own_tiles)
    own_row = pl.ds(me_c * own_tiles, own_tiles)

    def gather_row(j, source):
        part = pl.ds(source * own_tiles, own_tiles)
        return pltpu.make_async_remote_copy(
            src_ref=x_col.at[part], dst_ref=x_col.at[part],
            send_sem=agr_send.at[j], recv_sem=agr_recv.at[source],
            device_id=(j, me_c), device_id_type=MESH,
        )

    def gather_col(j, source):
        part = pl.ds(source * own_tiles, own_tiles)
        return pltpu.make_async_remote_copy(
            src_ref=x_row.at[part], dst_ref=x_row.at[part],
            send_sem=agc_send.at[j], recv_sem=agc_recv.at[source],
            device_id=(me_r, j), device_id_type=MESH,
        )

    def send_pieces(j, source, part, recv, send_sem, recv_sem, axis):
        return pltpu.make_async_remote_copy(
            src_ref=part, dst_ref=recv.at[source],
            send_sem=send_sem.at[j], recv_sem=recv_sem.at[source],
            device_id=(me_r, j) if axis == "col" else (j, me_c), device_id_type=MESH,
        )

    def f_send(j, source):
        return send_pieces(
            j, source, f_part.at[pl.ds(j * own_tiles, own_tiles)], f_recv, rsf_send, rsf_recv, "col")

    def b_send(j, source):
        return send_pieces(
            j, source, b_part.at[pl.ds(j * own_tiles, own_tiles)], b_recv, rsb_send, rsb_recv, "row")

    def df_send(j, source):
        return send_pieces(j, source, df_part.at[j], df_recv, dgf_send, dgf_recv, "col")

    def db_send(j, source):
        return send_pieces(j, source, db_part.at[j], db_recv, dgb_send, dgb_recv, "row")

    def d1_copy(j, source):
        return send_pieces(j, source, dots_row.at[me_r], dots_row, d1_send, d1_recv, "row")

    def d2_copy(j, source):
        return send_pieces(j, source, dots_col.at[me_c], dots_col, d2_send, d2_recv, "col")

    def start_gather():
        for t in range(own_tiles):
            piece = dir_ref[:, 128 * t : 128 * (t + 1)].astype(jnp.bfloat16)
            x_col[me_r * own_tiles + t] = piece
            x_row[me_c * own_tiles + t] = piece
        each_partner(n_row, me_r, lambda j: gather_row(j, me_r).start())
        each_partner(n_col, me_c, lambda j: gather_col(j, me_c).start())

    def forward_tile(row, weigh):
        fields, weights = [], []
        for i in range(PER_ROW):
            code = row_table[row * PER_ROW + i]
            fields.append(weigh(x_col, code & 63, col_tiles))
            weights.append(tiles[code >> 6])
        return lax.dot_general(
            jnp.concatenate(fields, axis=1), jnp.concatenate(weights, axis=1),
            (((1,), (1,)), ((), ())), preferred_element_type=jnp.float32)

    def backward_tile(col, weigh):
        fields, weights = [], []
        for i in range(per_col):
            code = col_table[col * per_col + i]
            fields.append(weigh(x_row, code & 127, row_tiles))
            weights.append(tiles[code >> 7])
        return jnp.dot(
            jnp.concatenate(fields, axis=1), jnp.concatenate(weights, axis=0),
            preferred_element_type=jnp.float32)

    def field_of(x_ref, index, limit):
        return x_ref[index]

    def ones_of(x_ref, index, limit):
        return ones[jnp.where(index == limit, 1, 0)]

    start_gather()
    for i in range(tile_sem.shape[0]):
        tile_copy(i).wait()

    def degree_group(n, own, tile_of, part, send):
        def one(k, carry):
            j = partner(own, k, n)
            for t in range(own_tiles):
                part[j, t : t + 1, :] = tile_of(j * own_tiles + t, ones_of)[0:1]
            part[j, own_tiles:, :] = jnp.zeros((8 - own_tiles, 128), jnp.float32)

            @pl.when(k != own_turn(n))
            def _():
                send(j, own).start()
            return carry

        lax.fori_loop(0, n, one, 0)

    degree_group(n_col, me_c, forward_tile, df_part, df_send)
    degree_group(n_row, me_r, backward_tile, db_part, db_send)

    def product_group(n, own, tile_of, part, send):
        def one(k, carry):
            j = partner(own, k, n)
            for t in range(own_tiles):
                part[j * own_tiles + t] = tile_of(j * own_tiles + t, field_of).astype(part.dtype)

            @pl.when(k != own_turn(n))
            def _():
                send(j, own).start()
            return carry

        lax.fori_loop(0, n, one, 0)

    def gather_sums(n, own, send, recv, totals):
        def one(k, sums):
            j = lax.rem(own + 1 + k, n)
            send(j, j).wait_recv()
            return tuple(s + recv[j, t].astype(jnp.float32) for t, s in enumerate(sums))

        return lax.fori_loop(0, n - 1, one, totals)

    lane = lax.broadcasted_iota(jnp.int32, (tasks, 128), 1)
    task = lax.broadcasted_iota(jnp.int32, (tasks, 128), 0)

    def one_step(step, carry):
        each_partner(n_row, me_r, lambda j: gather_row(j, j).wait_recv())
        product_group(n_col, me_c, forward_tile, f_part, f_send)
        each_partner(n_col, me_c, lambda j: gather_col(j, j).wait_recv())
        product_group(n_row, me_r, backward_tile, b_part, b_send)

        @pl.when(step == 0)
        def _():
            total = df_part[me_c] + db_part[me_r]
            def add_f(k, t):
                j = lax.rem(me_c + 1 + k, n_col)
                df_send(j, j).wait_recv()
                return t + df_recv[j]
            def add_b(k, t):
                j = lax.rem(me_r + 1 + k, n_row)
                db_send(j, j).wait_recv()
                return t + db_recv[j]
            total = lax.fori_loop(0, n_col - 1, add_f, total)
            total = lax.fori_loop(0, n_row - 1, add_b, total)
            degree[...] = 0.5 * total
            each_partner(n_col, me_c, lambda j: df_send(j, me_c).wait_send())
            each_partner(n_row, me_r, lambda j: db_send(j, me_r).wait_send())

        totals = tuple(
            f_part[me_c * own_tiles + t].astype(jnp.float32)
            + b_part[me_r * own_tiles + t].astype(jnp.float32)
            for t in range(own_tiles))
        totals = gather_sums(n_row, me_r, b_send, b_recv, totals)
        totals = gather_sums(n_col, me_c, f_send, f_recv, totals)

        pq = jnp.zeros((tasks, 128), jnp.float32)
        rq, qq, rr = pq, pq, pq
        images = []
        for t in range(own_tiles):
            part = slice(128 * t, 128 * (t + 1))
            p, r = dir_ref[:, part], res[:, part]
            q = p + coupling * (degree[t : t + 1, :] * p - 0.5 * totals[t])
            images.append(q)
            pq, rq, qq, rr = pq + p * q, rq + r * q, qq + q * q, rr + r * r
        row = jnp.zeros((tasks, 128), jnp.float32)
        for i, s in enumerate((pq, rq, qq, rr)):
            row = jnp.where(lane == task + tasks * i, jnp.sum(s, axis=1, keepdims=True), row)
        row = jnp.sum(row, axis=0, keepdims=True)
        dots_row[me_r] = jnp.broadcast_to(row, (8, 128))
        each_partner(n_row, me_r, lambda j: d1_copy(j, me_r).start())
        each_partner(n_row, me_r, lambda j: d1_copy(j, j).wait_recv())
        dots_col[me_c] = sum(dots_row[i] for i in range(n_row))
        each_partner(n_col, me_c, lambda j: d2_copy(j, me_c).start())
        each_partner(n_col, me_c, lambda j: d2_copy(j, j).wait_recv())
        sums = jnp.broadcast_to(sum(dots_col[i] for i in range(n_col))[0:1], (tasks, 128))
        pq, rq, qq, rr = (
            jnp.sum(jnp.where(lane == task + tasks * i, sums, 0.0), axis=1, keepdims=True)
            for i in range(4))
        size = rr / pq
        new = jnp.maximum(rr - 2.0 * size * rq + size * size * qq, 0.0)
        ratio = new / rr
        for t in range(own_tiles):
            part = slice(128 * t, 128 * (t + 1))
            p = dir_ref[:, part]
            r = res[:, part] - size * images[t]
            sol[:, part] = sol[:, part] + size * p
            res[:, part] = r
            dir_ref[:, part] = r + ratio * p

        each_partner(n_row, me_r, lambda j: gather_row(j, me_r).wait_send())
        each_partner(n_col, me_c, lambda j: gather_col(j, me_c).wait_send())
        each_partner(n_col, me_c, lambda j: f_send(j, me_c).wait_send())
        each_partner(n_row, me_r, lambda j: b_send(j, me_r).wait_send())
        each_partner(n_row, me_r, lambda j: d1_copy(j, me_r).wait_send())
        each_partner(n_col, me_c, lambda j: d2_copy(j, me_c).wait_send())

        @pl.when(step + 1 < ITERS)
        def _():
            start_gather()
        return carry

    lax.fori_loop(0, ITERS, one_step, 0)


def slot_table(own, other, live, per_tile, shift, empty):
    slot = jnp.arange(own.shape[0], dtype=jnp.int32)
    same = (own[:, None] == own[None, :]) & (slot[None, :] < slot[:, None])
    key = own * per_tile + jnp.sum(same.astype(jnp.int32), axis=1)
    code = (slot << shift) + jnp.where(live, other, empty)
    return jnp.sum(jnp.where(key[None, :] == slot[:, None], code[None, :], 0), axis=1)


def per_device(n_row, n_col, scores, tile_values, tile_rows, tile_cols, tile_count):
    tiles = tile_values[0, 0]
    rows, cols = tile_rows[0, 0], tile_cols[0, 0]
    slots = tiles.shape[0]
    tasks, piece = scores.shape
    own_tiles = piece // 128
    row_tiles, col_tiles = own_tiles * n_col, own_tiles * n_row
    per_col = slots // col_tiles
    live = jnp.arange(slots, dtype=jnp.int32) < tile_count[0, 0]
    row_table = slot_table(rows, cols, live, PER_ROW, 6, col_tiles)
    col_table = slot_table(cols, rows, live, per_col, 7, row_tiles)
    f32 = jnp.float32
    dma = pltpu.SemaphoreType.DMA
    vmem = pl.BlockSpec(memory_space=pltpu.VMEM)
    smem = pl.BlockSpec(memory_space=pltpu.SMEM)
    return pl.pallas_call(
        functools.partial(cg_kernel, n_row, n_col, per_col),
        out_shape=(
            jax.ShapeDtypeStruct((tasks, piece), f32),
            jax.ShapeDtypeStruct((tasks, piece), f32),
        ),
        in_specs=[smem, smem, vmem, pl.BlockSpec(memory_space=pl.ANY)],
        out_specs=(vmem, vmem),
        scratch_shapes=[
            pltpu.VMEM((slots, 128, 128), jnp.bfloat16),
            pltpu.VMEM((col_tiles + 1, tasks, 128), jnp.bfloat16),
            pltpu.VMEM((row_tiles + 1, tasks, 128), jnp.bfloat16),
            pltpu.VMEM((row_tiles, tasks, 128), SUM_TYPE),
            pltpu.VMEM((col_tiles, tasks, 128), SUM_TYPE),
            pltpu.VMEM((n_col, own_tiles, tasks, 128), SUM_TYPE),
            pltpu.VMEM((n_row, own_tiles, tasks, 128), SUM_TYPE),
            pltpu.VMEM((n_col, 8, 128), f32),
            pltpu.VMEM((n_row, 8, 128), f32),
            pltpu.VMEM((n_col, 8, 128), f32),
            pltpu.VMEM((n_row, 8, 128), f32),
            pltpu.VMEM((2, 16, 128), jnp.bfloat16),
            pltpu.VMEM((tasks, piece), f32),
            pltpu.VMEM((8, 128), f32),
            pltpu.VMEM((n_row, 8, 128), f32),
            pltpu.VMEM((n_col, 8, 128), f32),
            dma((8,)),
            dma((n_row,)), dma((n_row,)), dma((n_col,)), dma((n_col,)),
            dma((n_col,)), dma((n_col,)), dma((n_row,)), dma((n_row,)),
            dma((n_col,)), dma((n_col,)), dma((n_row,)), dma((n_row,)),
            dma((n_row,)), dma((n_row,)), dma((n_col,)), dma((n_col,)),
        ],
        compiler_params=pltpu.CompilerParams(
            collective_id=0, has_side_effects=True, vmem_limit_bytes=56 * 1024 * 1024
        ),
    )(row_table, col_table, scores, tiles)


def solution(mesh):
    return jax.shard_map(
        functools.partial(per_device, mesh.shape["row"], mesh.shape["col"]),
        mesh=mesh,
        in_specs=(
            P(None, ("row", "col")),
            P("row", "col", None, None, None),
            P("row", "col", None),
            P("row", "col", None),
            P("row", "col"),
        ),
        out_specs=(P(None, ("row", "col")), P(None, ("row", "col"))),
        check_vma=False,
    )
```

time: 1230 us -> 146 us (0.12); the launches traced: 1220 us -> 146 us
  blocking collectives: 432 us -> 0 us
  waiting for transfers between devices: 309 us -> 0 us
  other arithmetic: 297 us -> 4.24 us
  Pallas kernels: 0 us -> 137 us
  matrix products: 98.7 us -> 0 us
  local copies, waits for them, and re-layouts: 64 us -> 3.08 us
  between operations: 15.1 us -> 1.29 us
    psum x5 -> x0, blocking collectives: 318 us -> none  [inner_sums(): return lax.psum(parts, ('row', 'col'))]
    reduce_scatter x6 -> x0, waiting for transfers between devices: 309 us -> none  [the longest x3 230 us: to_rows(): lax.psum_scatter(partial_value, 'col', scatter_dimension=1, tiled=True)]
    scatter-add x32 -> x0, other arithmetic: 248 us -> none  [the longest x15 177 us: one_block(): forward_sum.at[:, rows_here, :].add(forward)]
    pallas_call x0 -> x1, Pallas kernels: none -> 137 us  [per_device(): pl.pallas_call(functools.partial(cg_kernel, n_row, n_col, per_col), out_s...]
    all_gather x6 -> x0, blocking collectives: 114 us -> none  [the longest x3 75.1 us: per_device(): graph_row_dir = lax.all_gather(graph_own_low, 'col', axis=1, tiled=True)]
    dot_general x30 -> x0, matrix products: 98.7 us -> none  [the longest x15 55.4 us: one_block(): jnp.einsum('ksd,sod->kso', col_pieces, tiles_here, preferred_element_type...]
    gather x30 -> x0, local copies, waits for them, and re-layouts: 38.3 us -> none  [the longest x15 27.7 us: one_block(): row_pieces = jnp.take(row_blocks, rows_here, axis=1)]
    and x15 -> x0, other arithmetic: 19.5 us -> none  [one_block(): row_pieces = jnp.take(row_blocks, rows_here, axis=1)]
  transfers between devices with their start and end apart: 8 -> 0, of which waited for: 6 -> 0; matrix products, arithmetic and copies ran while one was open for 13% -> 0% of each run, Pallas kernels for 0% -> 0%
where the time goes in v1:
time: 146 us
  Pallas kernels  137 us (94%)
  other arithmetic  4.24 us (3%)
  local copies, waits for them, and re-layouts  3.08 us (2%)
    pallas_call x1, Pallas kernels, per_device(): pl.pallas_call(functools.partial(cg_kernel, n_row, n_col, per_col), out_s...  137 us
    unnamed x2, local copies, waits for them, and re-layouts  3.08 us

profile of v1, /device:TPU:0, one launch (start us, length us, event | category | flops | bytes accessed | tf_op | source)
XLA Modules:
  0.0 145.8 jit_solution(3399881299032716102)
XLA Ops:
  1.3 1.0 convert_reduce_fusion.1
  2.3 1.0 convert_reduce_fusion
  3.3 0.7 select_add_fusion
  4.0 0.8 select_reduce_fusion.col_table
  4.8 0.8 select_reduce_fusion.1.row_table
  5.5 137.2 %shard_map.68 = (f32[32,768]{1,0:T(8,128)}, f32[32,768]{1,0:T(8,128)}) custom-call(s32[480]{0:T(512)} %select_reduce_fusion.1.row_table, s32[480]{0:T(512)} %select_reduce_fusion.col_table, f32[32,768]{1,0:T(8,128)} %scores.1, bf16[480,128,128]{2,1,0:T(8,128)(2,1)} %bitcast.5), custom_call_target="tpu_custom_call" | custom-call | tf_op jit(solution)/shard_map/pallas_call | solution.py:324
  142.7 1.5 %copy.10 = f32[32,768]{1,0:T(8,128)} copy(f32[32,768]{1,0:T(8,128)} %get-tuple-element.10) | data formatting | bytes 196608
  144.2 1.5 %copy.11 = f32[32,768]{1,0:T(8,128)} copy(f32[32,768]{1,0:T(8,128)} %get-tuple-element.11) | data formatting | bytes 196608

commit v2 on v1

--- a/solution.py
+++ b/solution.py
@@ -10,7 +10,8 @@
 PER_ROW = 5
 ITERS = 3
 MESH = pl.DeviceIdType.MESH
-SUM_TYPE = jnp.float32
+F_TYPE = jnp.bfloat16
+B_TYPE = jnp.float32
 
 coupling = 0.2
 
@@ -22,8 +23,9 @@
 
 def partner(me, k, n):
     slow, fast = spread(n)
-    a = lax.rem(me // fast + slow // 2 + k // fast, slow)
-    b = lax.rem(lax.rem(me, fast) + fast // 2 + lax.rem(k, fast), fast)
+    bits = fast.bit_length() - 1
+    a = ((me >> bits) + slow // 2 + (k >> bits)) & (slow - 1)
+    b = (me + fast // 2 + k) & (fast - 1)
     return a * fast + b
 
 
@@ -32,12 +34,34 @@
     return (slow - slow // 2) % slow * fast + (fast - fast // 2) % fast
 
 
+def slot_table(own, other, live, per_tile, shift, empty):
+    n = own.shape[1]
+    here = lax.broadcasted_iota(jnp.int32, (n, n), 0)
+    there = lax.broadcasted_iota(jnp.int32, (n, n), 1)
+
+    def down(line):
+        return jnp.sum(jnp.where(here == there, line, 0), axis=1, keepdims=True)
+
+    own_down, other_down = down(own), down(other)
+    earlier = (own_down == own) & (there < here)
+    key = own_down * per_tile + jnp.sum(jnp.where(earlier, 1, 0), axis=1, keepdims=True)
+    slot = here[:, :1]
+    code = (slot << shift) + jnp.where(slot < live, other_down, empty)
+    return jnp.sum(jnp.where(key == there, code, 0), axis=0, keepdims=True)
+
+
+def copy_kernel(sol_in, res_in, sol, res):
+    sol[...] = sol_in[...]
+    res[...] = res_in[...]
+
+
 def cg_kernel(
     n_row, n_col, per_col,
-    row_table, col_table, scores, tiles_hbm, sol, res,
+    count, rows, cols, scores, tiles_hbm, sol, res,
     tiles, x_col, x_row, f_part, b_part, f_recv, b_recv,
     df_part, db_part, df_recv, db_recv, ones, dir_ref, degree, dots_row, dots_col,
-    tile_sem,
+    row_codes, col_codes, row_table, col_table,
+    tile_sem, table_sem,
     agr_send, agr_recv, agc_send, agc_recv,
     rsf_send, rsf_recv, rsb_send, rsb_recv,
     dgf_send, dgf_recv, dgb_send, dgb_recv,
@@ -77,6 +101,15 @@
 
     x_col[col_tiles] = jnp.zeros((tasks, 128), jnp.bfloat16)
     x_row[row_tiles] = jnp.zeros((tasks, 128), jnp.bfloat16)
+    live = count[0, 0]
+    row_codes[...] = slot_table(rows[...], cols[...], live, PER_ROW, 6, col_tiles)
+    col_codes[...] = slot_table(cols[...], rows[...], live, per_col, 7, row_tiles)
+    table_copies = (
+        pltpu.make_async_copy(row_codes, row_table, table_sem.at[0]),
+        pltpu.make_async_copy(col_codes, col_table, table_sem.at[1]),
+    )
+    for copy in table_copies:
+        copy.start()
     ones[0] = jnp.ones((16, 128), jnp.bfloat16)
     ones[1] = jnp.zeros((16, 128), jnp.bfloat16)
     dir_ref[...] = scores[...]
@@ -151,7 +184,7 @@
     def forward_tile(row, weigh):
         fields, weights = [], []
         for i in range(PER_ROW):
-            code = row_table[row * PER_ROW + i]
+            code = row_table[0, row * PER_ROW + i]
             fields.append(weigh(x_col, code & 63, col_tiles))
             weights.append(tiles[code >> 6])
         return lax.dot_general(
@@ -161,7 +194,7 @@
     def backward_tile(col, weigh):
         fields, weights = [], []
         for i in range(per_col):
-            code = col_table[col * per_col + i]
+            code = col_table[0, col * per_col + i]
             fields.append(weigh(x_row, code & 127, row_tiles))
             weights.append(tiles[code >> 7])
         return jnp.dot(
@@ -171,46 +204,40 @@
     def field_of(x_ref, index, limit):
         return x_ref[index]
 
-    def ones_of(x_ref, index, limit):
-        return ones[jnp.where(index == limit, 1, 0)]
+    def field_and_ones(x_ref, index, limit):
+        unit = ones[jnp.where(index == limit, 1, 0)]
+        return jnp.concatenate([x_ref[index], unit], axis=0)
 
     start_gather()
     for i in range(tile_sem.shape[0]):
         tile_copy(i).wait()
 
-    def degree_group(n, own, tile_of, part, send):
+    for copy in table_copies:
+        copy.wait()
+
+    def product_group(n, own, tile_of, part, send, first, d_part, d_send):
         def one(k, carry):
             j = partner(own, k, n)
             for t in range(own_tiles):
-                part[j, t : t + 1, :] = tile_of(j * own_tiles + t, ones_of)[0:1]
-            part[j, own_tiles:, :] = jnp.zeros((8 - own_tiles, 128), jnp.float32)
+                product = tile_of(j * own_tiles + t, field_and_ones if first else field_of)
+                part[j * own_tiles + t] = product[:tasks].astype(part.dtype)
+                if first:
+                    d_part[j, t : t + 1, :] = product[tasks : tasks + 1]
+            if first:
+                d_part[j, own_tiles:, :] = jnp.zeros((8 - own_tiles, 128), jnp.float32)
 
             @pl.when(k != own_turn(n))
             def _():
                 send(j, own).start()
-            return carry
-
-        lax.fori_loop(0, n, one, 0)
-
-    degree_group(n_col, me_c, forward_tile, df_part, df_send)
-    degree_group(n_row, me_r, backward_tile, db_part, db_send)
-
-    def product_group(n, own, tile_of, part, send):
-        def one(k, carry):
-            j = partner(own, k, n)
-            for t in range(own_tiles):
-                part[j * own_tiles + t] = tile_of(j * own_tiles + t, field_of).astype(part.dtype)
-
-            @pl.when(k != own_turn(n))
-            def _():
-                send(j, own).start()
+                if first:
+                    d_send(j, own).start()
             return carry
 
         lax.fori_loop(0, n, one, 0)
 
     def gather_sums(n, own, send, recv, totals):
         def one(k, sums):
-            j = lax.rem(own + 1 + k, n)
+            j = (own + 1 + k) & (n - 1)
             send(j, j).wait_recv()
             return tuple(s + recv[j, t].astype(jnp.float32) for t, s in enumerate(sums))
 
@@ -219,28 +246,28 @@
     lane = lax.broadcasted_iota(jnp.int32, (tasks, 128), 1)
     task = lax.broadcasted_iota(jnp.int32, (tasks, 128), 0)
 
-    def one_step(step, carry):
+    def one_step(step, first):
         each_partner(n_row, me_r, lambda j: gather_row(j, j).wait_recv())
-        product_group(n_col, me_c, forward_tile, f_part, f_send)
+        product_group(n_col, me_c, forward_tile, f_part, f_send, first, df_part, df_send)
         each_partner(n_col, me_c, lambda j: gather_col(j, j).wait_recv())
-        product_group(n_row, me_r, backward_tile, b_part, b_send)
-
-        @pl.when(step == 0)
-        def _():
+        product_group(n_row, me_r, backward_tile, b_part, b_send, first, db_part, db_send)
+
+        if first:
             total = df_part[me_c] + db_part[me_r]
+
             def add_f(k, t):
-                j = lax.rem(me_c + 1 + k, n_col)
+                j = (me_c + 1 + k) & (n_col - 1)
                 df_send(j, j).wait_recv()
                 return t + df_recv[j]
+
             def add_b(k, t):
-                j = lax.rem(me_r + 1 + k, n_row)
+                j = (me_r + 1 + k) & (n_row - 1)
                 db_send(j, j).wait_recv()
                 return t + db_recv[j]
+
+            total = lax.fori_loop(0, n_row - 1, add_b, total)
             total = lax.fori_loop(0, n_col - 1, add_f, total)
-            total = lax.fori_loop(0, n_row - 1, add_b, total)
             degree[...] = 0.5 * total
-            each_partner(n_col, me_c, lambda j: df_send(j, me_c).wait_send())
-            each_partner(n_row, me_r, lambda j: db_send(j, me_r).wait_send())
 
         totals = tuple(
             f_part[me_c * own_tiles + t].astype(jnp.float32)
@@ -290,53 +317,51 @@
         each_partner(n_row, me_r, lambda j: d1_copy(j, me_r).wait_send())
         each_partner(n_col, me_c, lambda j: d2_copy(j, me_c).wait_send())
 
+        if first:
+            each_partner(n_col, me_c, lambda j: df_send(j, me_c).wait_send())
+            each_partner(n_row, me_r, lambda j: db_send(j, me_r).wait_send())
+
         @pl.when(step + 1 < ITERS)
         def _():
             start_gather()
+
+    one_step(0, True)
+
+    def later_step(step, carry):
+        one_step(step, False)
         return carry
 
-    lax.fori_loop(0, ITERS, one_step, 0)
-
-
-def slot_table(own, other, live, per_tile, shift, empty):
-    slot = jnp.arange(own.shape[0], dtype=jnp.int32)
-    same = (own[:, None] == own[None, :]) & (slot[None, :] < slot[:, None])
-    key = own * per_tile + jnp.sum(same.astype(jnp.int32), axis=1)
-    code = (slot << shift) + jnp.where(live, other, empty)
-    return jnp.sum(jnp.where(key[None, :] == slot[:, None], code[None, :], 0), axis=1)
+    lax.fori_loop(1, ITERS, later_step, 0)
 
 
 def per_device(n_row, n_col, scores, tile_values, tile_rows, tile_cols, tile_count):
     tiles = tile_values[0, 0]
-    rows, cols = tile_rows[0, 0], tile_cols[0, 0]
+    rows, cols = tile_rows[0], tile_cols[0]
     slots = tiles.shape[0]
     tasks, piece = scores.shape
     own_tiles = piece // 128
     row_tiles, col_tiles = own_tiles * n_col, own_tiles * n_row
     per_col = slots // col_tiles
-    live = jnp.arange(slots, dtype=jnp.int32) < tile_count[0, 0]
-    row_table = slot_table(rows, cols, live, PER_ROW, 6, col_tiles)
-    col_table = slot_table(cols, rows, live, per_col, 7, row_tiles)
     f32 = jnp.float32
     dma = pltpu.SemaphoreType.DMA
     vmem = pl.BlockSpec(memory_space=pltpu.VMEM)
     smem = pl.BlockSpec(memory_space=pltpu.SMEM)
-    return pl.pallas_call(
+    sol, res = pl.pallas_call(
         functools.partial(cg_kernel, n_row, n_col, per_col),
         out_shape=(
             jax.ShapeDtypeStruct((tasks, piece), f32),
             jax.ShapeDtypeStruct((tasks, piece), f32),
         ),
-        in_specs=[smem, smem, vmem, pl.BlockSpec(memory_space=pl.ANY)],
+        in_specs=[smem, vmem, vmem, vmem, pl.BlockSpec(memory_space=pl.ANY)],
         out_specs=(vmem, vmem),
         scratch_shapes=[
             pltpu.VMEM((slots, 128, 128), jnp.bfloat16),
             pltpu.VMEM((col_tiles + 1, tasks, 128), jnp.bfloat16),
             pltpu.VMEM((row_tiles + 1, tasks, 128), jnp.bfloat16),
-            pltpu.VMEM((row_tiles, tasks, 128), SUM_TYPE),
-            pltpu.VMEM((col_tiles, tasks, 128), SUM_TYPE),
-            pltpu.VMEM((n_col, own_tiles, tasks, 128), SUM_TYPE),
-            pltpu.VMEM((n_row, own_tiles, tasks, 128), SUM_TYPE),
+            pltpu.VMEM((row_tiles, tasks, 128), F_TYPE),
+            pltpu.VMEM((col_tiles, tasks, 128), B_TYPE),
+            pltpu.VMEM((n_col, own_tiles, tasks, 128), F_TYPE),
+            pltpu.VMEM((n_row, own_tiles, tasks, 128), B_TYPE),
             pltpu.VMEM((n_col, 8, 128), f32),
             pltpu.VMEM((n_row, 8, 128), f32),
             pltpu.VMEM((n_col, 8, 128), f32),
@@ -346,7 +371,11 @@
             pltpu.VMEM((8, 128), f32),
             pltpu.VMEM((n_row, 8, 128), f32),
             pltpu.VMEM((n_col, 8, 128), f32),
-            dma((8,)),
+            pltpu.VMEM((1, slots), jnp.int32),
+            pltpu.VMEM((1, slots), jnp.int32),
+            pltpu.SMEM((1, slots), jnp.int32),
+            pltpu.SMEM((1, slots), jnp.int32),
+            dma((8,)), dma((2,)),
             dma((n_row,)), dma((n_row,)), dma((n_col,)), dma((n_col,)),
             dma((n_col,)), dma((n_col,)), dma((n_row,)), dma((n_row,)),
             dma((n_col,)), dma((n_col,)), dma((n_row,)), dma((n_row,)),
@@ -355,7 +384,16 @@
         compiler_params=pltpu.CompilerParams(
             collective_id=0, has_side_effects=True, vmem_limit_bytes=56 * 1024 * 1024
         ),
-    )(row_table, col_table, scores, tiles)
+    )(tile_count, rows, cols, scores, tiles)
+    return pl.pallas_call(
+        copy_kernel,
+        out_shape=(
+            jax.ShapeDtypeStruct((tasks, piece), f32),
+            jax.ShapeDtypeStruct((tasks, piece), f32),
+        ),
+        in_specs=[vmem, vmem],
+        out_specs=(vmem, vmem),
+    )(sol, res)
 
 
 def solution(mesh):

time: 146 us -> 119 us (0.82)
  Pallas kernels: 137 us -> 117 us
  other arithmetic: 4.24 us -> 0 us
  local copies, waits for them, and re-layouts: 3.08 us -> 0 us
    pallas_call x1, Pallas kernels: 137 us -> 115 us  [per_device(): pl.pallas_call(functools.partial(cg_kernel, n_row, n_col, per_col), out_s...]
    reduce_sum x4 -> x0, other arithmetic: 3.53 us -> none  [the longest x2 2 us: slot_table(): key = own * per_tile + jnp.sum(same.astype(jnp.int32), axis=1)]
    unnamed x2 -> x0, local copies, waits for them, and re-layouts: 3.08 us -> none
    pallas_call x0 -> x1, Pallas kernels: none -> 1.62 us  [per_device(): pl.pallas_call(copy_kernel, out_shape=(jax.ShapeDtypeStruct((tasks, piece...]
where the time goes in v2:
time: 119 us; the launch traced here: 118 us
  Pallas kernels  117 us (98%)
  between operations  1.29 us (1%)
    pallas_call x1, Pallas kernels, per_device(): pl.pallas_call(functools.partial(cg_kernel, n_row, n_col, per_col), out_s...  115 us

profile of v2, /device:TPU:0, one launch (start us, length us, event | category | flops | bytes accessed | tf_op | source)
XLA Modules:
  0.0 118.3 jit_solution(1353894323448447431)
XLA Ops:
  1.3 115.4 %shard_map.68 = (f32[32,768]{1,0:T(8,128)}, f32[32,768]{1,0:T(8,128)}) custom-call(s32[1,1]{1,0:T(1,128)S(6)} %copy.7.count, s32[1,480]{1,0:T(1,128)} %bitcast.4, s32[1,480]{1,0:T(1,128)} %bitcast.5, f32[32,768]{1,0:T(8,128)} %scores.1, bf16[480,128,128]{2,1,0:T(8,128)(2,1)} %bitcast.3), custom_call_target="tpu_custom_call" | custom-call | tf_op jit(solution)/shard_map/pallas_call | solution.py:349
  116.7 1.6 %shard_map.69 = (f32[32,768]{1,0:T(8,128)}, f32[32,768]{1,0:T(8,128)}) custom-call(f32[32,768]{1,0:T(8,128)} %get-tuple-element.4.sol_in, f32[32,768]{1,0:T(8,128)} %get-tuple-element.5.res_in), custom_call_target="tpu_custom_call" | custom-call | tf_op jit(solution)/shard_map/pallas_call | solution.py:388

commit v3 on v2

--- a/solution.py
+++ b/solution.py
@@ -55,20 +55,31 @@
     res[...] = res_in[...]
 
 
+def pick(index, values):
+    value = values[-1]
+    for i, v in enumerate(values[:-1]):
+        value = jnp.where(index == i, v, value)
+    return value
+
+
 def cg_kernel(
     n_row, n_col, per_col,
     count, rows, cols, scores, tiles_hbm, sol, res,
-    tiles, x_col, x_row, f_part, b_part, f_recv, b_recv,
+    tiles, x_col, x_row, f_part, b_part, f_recv, b_recv, pair,
     df_part, db_part, df_recv, db_recv, ones, dir_ref, degree, dots_row, dots_col,
     row_codes, col_codes, row_table, col_table,
     tile_sem, table_sem,
     agr_send, agr_recv, agc_send, agc_recv,
-    rsf_send, rsf_recv, rsb_send, rsb_recv,
+    rsf_send, rsf_recv, rsb_send, rsb_recv, pair_send, pair_recv,
     dgf_send, dgf_recv, dgb_send, dgb_recv,
     d1_send, d1_recv, d2_send, d2_recv,
 ):
     me_r = lax.axis_index("row")
     me_c = lax.axis_index("col")
+    y, core = me_r >> 1, me_r & 1
+    chips = n_row // 2
+    sibling = me_r + 1 - 2 * core
+    far_first = sorted(range(1, chips), key=lambda d: -min(d, chips - d))
     tasks = scores.shape[0]
     own_tiles = scores.shape[1] // 128
     slots = tiles.shape[0]
@@ -130,13 +141,16 @@
     own_col = pl.ds(me_r * own_tiles, own_tiles)
     own_row = pl.ds(me_c * own_tiles, own_tiles)
 
-    def gather_row(j, source):
+    def gather_row(j, source, sem):
         part = pl.ds(source * own_tiles, own_tiles)
         return pltpu.make_async_remote_copy(
             src_ref=x_col.at[part], dst_ref=x_col.at[part],
-            send_sem=agr_send.at[j], recv_sem=agr_recv.at[source],
+            send_sem=agr_send.at[sem], recv_sem=agr_recv.at[source],
             device_id=(j, me_c), device_id_type=MESH,
         )
+
+    def at_chip(d, on_core):
+        return ((y + d) & (chips - 1)) * 2 + on_core
 
     def gather_col(j, source):
         part = pl.ds(source * own_tiles, own_tiles)
@@ -157,9 +171,29 @@
         return send_pieces(
             j, source, f_part.at[pl.ds(j * own_tiles, own_tiles)], f_recv, rsf_send, rsf_recv, "col")
 
-    def b_send(j, source):
-        return send_pieces(
-            j, source, b_part.at[pl.ds(j * own_tiles, own_tiles)], b_recv, rsb_send, rsb_recv, "row")
+    def b_send(d):
+        j = at_chip(d, core)
+        return pltpu.make_async_remote_copy(
+            src_ref=b_part.at[pl.ds(j * own_tiles, own_tiles)], dst_ref=b_recv.at[y],
+            send_sem=rsb_send.at[d], recv_sem=rsb_recv.at[y],
+            device_id=(j, me_c), device_id_type=MESH,
+        )
+
+    def b_arrival(d):
+        source = (y + d) & (chips - 1)
+        return pltpu.make_async_remote_copy(
+            src_ref=b_part.at[pl.ds(me_r * own_tiles, own_tiles)], dst_ref=b_recv.at[source],
+            send_sem=rsb_send.at[d], recv_sem=rsb_recv.at[source],
+            device_id=(at_chip(d, core), me_c), device_id_type=MESH,
+        )
+
+    def pair_copy(d):
+        j = at_chip(d, 1 - core)
+        return pltpu.make_async_remote_copy(
+            src_ref=b_part.at[pl.ds(j * own_tiles, own_tiles)], dst_ref=pair.at[d],
+            send_sem=pair_send.at[d], recv_sem=pair_recv.at[d],
+            device_id=(sibling, me_c), device_id_type=MESH,
+        )
 
     def df_send(j, source):
         return send_pieces(j, source, df_part.at[j], df_recv, dgf_send, dgf_recv, "col")
@@ -178,8 +212,27 @@
             piece = dir_ref[:, 128 * t : 128 * (t + 1)].astype(jnp.bfloat16)
             x_col[me_r * own_tiles + t] = piece
             x_row[me_c * own_tiles + t] = piece
-        each_partner(n_row, me_r, lambda j: gather_row(j, me_r).start())
+        for d in far_first:
+            gather_row(at_chip(d, core), me_r, at_chip(d, core)).start()
+        gather_row(sibling, me_r, sibling).start()
         each_partner(n_col, me_c, lambda j: gather_col(j, me_c).start())
+
+    def pass_row_on():
+        for d in reversed(far_first):
+            source = at_chip(d, core)
+            gather_row(source, source, source).wait_recv()
+            gather_row(sibling, source, at_chip(d, 1 - core)).start()
+        gather_row(sibling, sibling, sibling).wait_recv()
+        for d in reversed(far_first):
+            source = at_chip(d, 1 - core)
+            gather_row(sibling, source, source).wait_recv()
+
+    def end_gather_sends():
+        for d in far_first:
+            gather_row(at_chip(d, core), me_r, at_chip(d, core)).wait_send()
+            gather_row(sibling, at_chip(d, core), at_chip(d, 1 - core)).wait_send()
+        gather_row(sibling, me_r, sibling).wait_send()
+        each_partner(n_col, me_c, lambda j: gather_col(j, me_c).wait_send())
 
     def forward_tile(row, weigh):
         fields, weights = [], []
@@ -215,25 +268,66 @@
     for copy in table_copies:
         copy.wait()
 
-    def product_group(n, own, tile_of, part, send, first, d_part, d_send):
+    def chunk_products(j, tile_of, part, first, d_part):
+        for t in range(own_tiles):
+            product = tile_of(j * own_tiles + t, field_and_ones if first else field_of)
+            part[j * own_tiles + t] = product[:tasks].astype(part.dtype)
+            if first:
+                d_part[j, t : t + 1, :] = product[tasks : tasks + 1]
+        if first:
+            d_part[j, own_tiles:, :] = jnp.zeros((8 - own_tiles, 128), jnp.float32)
+
+    def forward_products(first):
         def one(k, carry):
-            j = partner(own, k, n)
-            for t in range(own_tiles):
-                product = tile_of(j * own_tiles + t, field_and_ones if first else field_of)
-                part[j * own_tiles + t] = product[:tasks].astype(part.dtype)
+            j = partner(me_c, k, n_col)
+            chunk_products(j, forward_tile, f_part, first, df_part)
+
+            @pl.when(k != own_turn(n_col))
+            def _():
+                f_send(j, me_c).start()
                 if first:
-                    d_part[j, t : t + 1, :] = product[tasks : tasks + 1]
+                    df_send(j, me_c).start()
+            return carry
+
+        lax.fori_loop(0, n_col, one, 0)
+
+    turns = far_first + [0]
+    ahead = [(d, 0) for d in turns]
+    behind = [(d, 1) for d in turns]
+    order = [ahead[0]]
+    for i in range(1, chips):
+        order += [ahead[i], behind[i - 1]]
+    order.append(behind[-1])
+
+    def backward_products(first):
+        def one(k, carry):
+            d = pick(k, [d for d, final in order])
+            final = pick(k, [final for d, final in order])
+            j = at_chip(d, core + (1 - final) * (1 - 2 * core))
+            chunk_products(j, backward_tile, b_part, first, db_part)
+
+            @pl.when(final == 0)
+            def _():
+                pair_copy(d).start()
+
+            @pl.when(final == 1)
+            def _():
+                pair_copy(d).wait_recv()
+                for t in range(own_tiles):
+                    b_part[j * own_tiles + t] = b_part[j * own_tiles + t] + pair[d, t]
+
+                @pl.when(d != 0)
+                def _():
+                    b_send(d).start()
+
             if first:
-                d_part[j, own_tiles:, :] = jnp.zeros((8 - own_tiles, 128), jnp.float32)
-
-            @pl.when(k != own_turn(n))
-            def _():
-                send(j, own).start()
-                if first:
-                    d_send(j, own).start()
+
+                @pl.when(j != me_r)
+                def _():
+                    db_send(j, me_r).start()
             return carry
 
-        lax.fori_loop(0, n, one, 0)
+        lax.fori_loop(0, n_row, one, 0)
 
     def gather_sums(n, own, send, recv, totals):
         def one(k, sums):
@@ -247,10 +341,11 @@
     task = lax.broadcasted_iota(jnp.int32, (tasks, 128), 0)
 
     def one_step(step, first):
-        each_partner(n_row, me_r, lambda j: gather_row(j, j).wait_recv())
-        product_group(n_col, me_c, forward_tile, f_part, f_send, first, df_part, df_send)
+        pass_row_on()
+        forward_products(first)
         each_partner(n_col, me_c, lambda j: gather_col(j, j).wait_recv())
-        product_group(n_row, me_r, backward_tile, b_part, b_send, first, db_part, db_send)
+        backward_products(first)
+        end_gather_sends()
 
         if first:
             total = df_part[me_c] + db_part[me_r]
@@ -273,8 +368,11 @@
             f_part[me_c * own_tiles + t].astype(jnp.float32)
             + b_part[me_r * own_tiles + t].astype(jnp.float32)
             for t in range(own_tiles))
-        totals = gather_sums(n_row, me_r, b_send, b_recv, totals)
         totals = gather_sums(n_col, me_c, f_send, f_recv, totals)
+        for d in reversed(far_first):
+            b_arrival(d).wait_recv()
+            source = (y + d) & (chips - 1)
+            totals = tuple(s + b_recv[source, t] for t, s in enumerate(totals))
 
         pq = jnp.zeros((tasks, 128), jnp.float32)
         rq, qq, rr = pq, pq, pq
@@ -289,41 +387,45 @@
         for i, s in enumerate((pq, rq, qq, rr)):
             row = jnp.where(lane == task + tasks * i, jnp.sum(s, axis=1, keepdims=True), row)
         row = jnp.sum(row, axis=0, keepdims=True)
-        dots_row[me_r] = jnp.broadcast_to(row, (8, 128))
+        dots_row[me_r] = row
         each_partner(n_row, me_r, lambda j: d1_copy(j, me_r).start())
         each_partner(n_row, me_r, lambda j: d1_copy(j, j).wait_recv())
         dots_col[me_c] = sum(dots_row[i] for i in range(n_row))
         each_partner(n_col, me_c, lambda j: d2_copy(j, me_c).start())
         each_partner(n_col, me_c, lambda j: d2_copy(j, j).wait_recv())
-        sums = jnp.broadcast_to(sum(dots_col[i] for i in range(n_col))[0:1], (tasks, 128))
+        sums = jnp.broadcast_to(sum(dots_col[i] for i in range(n_col)), (tasks, 128))
         pq, rq, qq, rr = (
             jnp.sum(jnp.where(lane == task + tasks * i, sums, 0.0), axis=1, keepdims=True)
             for i in range(4))
         size = rr / pq
         new = jnp.maximum(rr - 2.0 * size * rq + size * size * qq, 0.0)
         ratio = new / rr
+        moves = []
         for t in range(own_tiles):
             part = slice(128 * t, 128 * (t + 1))
             p = dir_ref[:, part]
             r = res[:, part] - size * images[t]
-            sol[:, part] = sol[:, part] + size * p
+            moves.append(size * p)
             res[:, part] = r
             dir_ref[:, part] = r + ratio * p
 
-        each_partner(n_row, me_r, lambda j: gather_row(j, me_r).wait_send())
-        each_partner(n_col, me_c, lambda j: gather_col(j, me_c).wait_send())
+        @pl.when(step + 1 < ITERS)
+        def _():
+            start_gather()
+
+        for t in range(own_tiles):
+            part = slice(128 * t, 128 * (t + 1))
+            sol[:, part] = sol[:, part] + moves[t]
         each_partner(n_col, me_c, lambda j: f_send(j, me_c).wait_send())
-        each_partner(n_row, me_r, lambda j: b_send(j, me_r).wait_send())
+        for d in range(chips):
+            pair_copy(d).wait_send()
+        for d in far_first:
+            b_send(d).wait_send()
         each_partner(n_row, me_r, lambda j: d1_copy(j, me_r).wait_send())
         each_partner(n_col, me_c, lambda j: d2_copy(j, me_c).wait_send())
-
         if first:
             each_partner(n_col, me_c, lambda j: df_send(j, me_c).wait_send())
             each_partner(n_row, me_r, lambda j: db_send(j, me_r).wait_send())
-
-        @pl.when(step + 1 < ITERS)
-        def _():
-            start_gather()
 
     one_step(0, True)
 
@@ -361,7 +463,8 @@
             pltpu.VMEM((row_tiles, tasks, 128), F_TYPE),
             pltpu.VMEM((col_tiles, tasks, 128), B_TYPE),
             pltpu.VMEM((n_col, own_tiles, tasks, 128), F_TYPE),
-            pltpu.VMEM((n_row, own_tiles, tasks, 128), B_TYPE),
+            pltpu.VMEM((n_row // 2, own_tiles, tasks, 128), B_TYPE),
+            pltpu.VMEM((n_row // 2, own_tiles, tasks, 128), B_TYPE),
             pltpu.VMEM((n_col, 8, 128), f32),
             pltpu.VMEM((n_row, 8, 128), f32),
             pltpu.VMEM((n_col, 8, 128), f32),
@@ -369,15 +472,16 @@
             pltpu.VMEM((2, 16, 128), jnp.bfloat16),
             pltpu.VMEM((tasks, piece), f32),
             pltpu.VMEM((8, 128), f32),
-            pltpu.VMEM((n_row, 8, 128), f32),
-            pltpu.VMEM((n_col, 8, 128), f32),
+            pltpu.VMEM((n_row, 1, 128), f32),
+            pltpu.VMEM((n_col, 1, 128), f32),
             pltpu.VMEM((1, slots), jnp.int32),
             pltpu.VMEM((1, slots), jnp.int32),
             pltpu.SMEM((1, slots), jnp.int32),
             pltpu.SMEM((1, slots), jnp.int32),
             dma((8,)), dma((2,)),
             dma((n_row,)), dma((n_row,)), dma((n_col,)), dma((n_col,)),
-            dma((n_col,)), dma((n_col,)), dma((n_row,)), dma((n_row,)),
+            dma((n_col,)), dma((n_col,)), dma((n_row // 2,)), dma((n_row // 2,)),
+            dma((n_row // 2,)), dma((n_row // 2,)),
             dma((n_col,)), dma((n_col,)), dma((n_row,)), dma((n_row,)),
             dma((n_row,)), dma((n_row,)), dma((n_col,)), dma((n_col,)),
         ],

time: 119 us -> 107 us (0.90)
  Pallas kernels: 117 us -> 105 us
    pallas_call x1, Pallas kernels: 115 us -> 104 us  [per_device(): pl.pallas_call(functools.partial(cg_kernel, n_row, n_col, per_col), out_s...]
where the time goes in v3:
time: 107 us; the launch traced here: 106 us
  Pallas kernels  105 us (98%)
  between operations  1.29 us (1%)
    pallas_call x1, Pallas kernels, per_device(): pl.pallas_call(functools.partial(cg_kernel, n_row, n_col, per_col), out_s...  104 us

profile of v3, /device:TPU:0, one launch (start us, length us, event | category | flops | bytes accessed | tf_op | source)
XLA Modules:
  0.0 106.4 jit_solution(8217490701585230688)
XLA Ops:
  1.3 103.5 %shard_map.68 = (f32[32,768]{1,0:T(8,128)}, f32[32,768]{1,0:T(8,128)}) custom-call(s32[1,1]{1,0:T(1,128)S(6)} %copy.7.count, s32[1,480]{1,0:T(1,128)} %bitcast.4, s32[1,480]{1,0:T(1,128)} %bitcast.5, f32[32,768]{1,0:T(8,128)} %scores.1, bf16[480,128,128]{2,1,0:T(8,128)(2,1)} %bitcast.3), custom_call_target="tpu_custom_call" | custom-call | tf_op jit(solution)/shard_map/pallas_call | solution.py:451
  104.8 1.6 %shard_map.69 = (f32[32,768]{1,0:T(8,128)}, f32[32,768]{1,0:T(8,128)}) custom-call(f32[32,768]{1,0:T(8,128)} %get-tuple-element.4.sol_in, f32[32,768]{1,0:T(8,128)} %get-tuple-element.5.res_in), custom_call_target="tpu_custom_call" | custom-call | tf_op jit(solution)/shard_map/pallas_call | solution.py:492

commit v4 on v3

v4 whole, which is shorter than its diff:
```python
import functools

import jax
import jax.numpy as jnp
from jax import lax
from jax.experimental import pallas as pl
from jax.experimental.pallas import tpu as pltpu
from jax.sharding import PartitionSpec as P

PER_ROW = 5
ITERS = 3
MESH = pl.DeviceIdType.MESH
F_TYPE = jnp.bfloat16
B_TYPE = jnp.float32

coupling = 0.2


def spread(n):
    fast = 2 if n <= 8 else 4
    return n // fast, fast


def partner(me, k, n):
    slow, fast = spread(n)
    bits = fast.bit_length() - 1
    a = ((me >> bits) + slow // 2 + (k >> bits)) & (slow - 1)
    b = (me + fast // 2 + k) & (fast - 1)
    return a * fast + b


def own_turn(n):
    slow, fast = spread(n)
    return (slow - slow // 2) % slow * fast + (fast - fast // 2) % fast


def slot_table(own, other, live, per_tile, shift, empty):
    n = own.shape[1]
    here = lax.broadcasted_iota(jnp.int32, (n, n), 0)
    there = lax.broadcasted_iota(jnp.int32, (n, n), 1)

    def down(line):
        return jnp.sum(jnp.where(here == there, line, 0), axis=1, keepdims=True)

    own_down, other_down = down(own), down(other)
    earlier = (own_down == own) & (there < here)
    key = own_down * per_tile + jnp.sum(jnp.where(earlier, 1, 0), axis=1, keepdims=True)
    slot = here[:, :1]
    code = (slot << shift) + jnp.where(slot < live, other_down, empty)
    return jnp.sum(jnp.where(key == there, code, 0), axis=0, keepdims=True)


def copy_kernel(sol_in, res_in, sol, res):
    sol[...] = sol_in[...]
    res[...] = res_in[...]


def pick(index, values):
    value = values[-1]
    for i, v in enumerate(values[:-1]):
        value = jnp.where(index == i, v, value)
    return value


def cg_kernel(
    n_row, n_col, per_col,
    count, rows, cols, scores, tiles_hbm, sol, res,
    tiles, x_col, x_row, f_part, b_part, f_recv, b_recv, pair,
    df_part, db_part, df_recv, db_recv, ones, dir_ref, degree, dots_row, dots_col,
    row_codes, col_codes, row_table, col_table,
    tile_sem, table_sem,
    agr_send, agr_recv, agc_send, agc_recv,
    rsf_send, rsf_recv, rsb_send, rsb_recv, pair_send, pair_recv,
    dgf_send, dgf_recv, dgb_send, dgb_recv,
    d1_send, d1_recv, d2_send, d2_recv,
):
    me_r = lax.axis_index("row")
    me_c = lax.axis_index("col")
    y, core = me_r >> 1, me_r & 1
    chips = n_row // 2
    sibling = me_r + 1 - 2 * core
    far_first = sorted(range(1, chips), key=lambda d: -min(d, chips - d))
    tasks = scores.shape[0]
    own_tiles = scores.shape[1] // 128
    slots = tiles.shape[0]
    col_tiles = b_part.shape[0]
    row_tiles = f_part.shape[0]
    chunk = slots // tile_sem.shape[0]

    def tile_copy(i):
        part = pl.ds(i * chunk, chunk)
        return pltpu.make_async_copy(tiles_hbm.at[part], tiles.at[part], tile_sem.at[i])

    for i in range(tile_sem.shape[0]):
        tile_copy(i).start()

    barrier = pltpu.get_barrier_semaphore()

    def greet(axis, n, own):
        def one(k, carry):
            @pl.when(k != own_turn(n))
            def _():
                j = partner(own, k, n)
                target = (me_r, j) if axis == "col" else (j, me_c)
                pl.semaphore_signal(barrier, inc=1, device_id=target, device_id_type=MESH)
            return carry

        lax.fori_loop(0, n, one, 0)

    greet("col", n_col, me_c)
    greet("row", n_row, me_r)

    x_col[col_tiles] = jnp.zeros((tasks, 128), jnp.bfloat16)
    x_row[row_tiles] = jnp.zeros((tasks, 128), jnp.bfloat16)
    ones[0] = jnp.ones((16, 128), jnp.bfloat16)
    ones[1] = jnp.zeros((16, 128), jnp.bfloat16)
    dir_ref[...] = scores[...]
    res[...] = scores[...]
    sol[...] = jnp.zeros_like(sol)

    pl.semaphore_wait(barrier, n_row + n_col - 2)

    def each_partner(n, own, action):
        def one(k, carry):
            @pl.when(k != own_turn(n))
            def _():
                action(partner(own, k, n))
            return carry

        lax.fori_loop(0, n, one, 0)

    own_col = pl.ds(me_r * own_tiles, own_tiles)
    own_row = pl.ds(me_c * own_tiles, own_tiles)

    def gather_row(j, source, sem):
        part = pl.ds(source * own_tiles, own_tiles)
        return pltpu.make_async_remote_copy(
            src_ref=x_col.at[part], dst_ref=x_col.at[part],
            send_sem=agr_send.at[sem], recv_sem=agr_recv.at[source],
            device_id=(j, me_c), device_id_type=MESH,
        )

    def all_of(ref, number, send_sem, recv_sem):
        part = ref.at[pl.ds(0, number)]
        return pltpu.make_async_remote_copy(
            src_ref=part, dst_ref=part, send_sem=send_sem.at[0], recv_sem=recv_sem.at[0],
            device_id=(sibling, me_c), device_id_type=MESH,
        )

    others_row, others_col = n_row - 1, n_col - 1
    all_cols = all_of(x_row, others_col * own_tiles, agc_send, agc_recv)
    all_f = all_of(f_part, others_col * own_tiles, rsf_send, rsf_send)
    all_df = all_of(df_recv, others_col, dgf_send, dgf_recv)
    all_db = all_of(db_recv, others_row, dgb_send, dgb_recv)
    all_d1 = all_of(dots_row, others_row, d1_send, d1_recv)
    all_d2 = all_of(dots_col, others_col, d2_send, d2_recv)

    def at_chip(d, on_core):
        return ((y + d) & (chips - 1)) * 2 + on_core

    def gather_col(j, source):
        part = pl.ds(source * own_tiles, own_tiles)
        return pltpu.make_async_remote_copy(
            src_ref=x_row.at[part], dst_ref=x_row.at[part],
            send_sem=agc_send.at[0], recv_sem=agc_recv.at[0],
            device_id=(me_r, j), device_id_type=MESH,
        )

    def send_pieces(j, source, part, recv, send_sem, recv_sem, axis):
        return pltpu.make_async_remote_copy(
            src_ref=part, dst_ref=recv.at[source],
            send_sem=send_sem.at[0], recv_sem=recv_sem.at[source if recv is f_recv else 0],
            device_id=(me_r, j) if axis == "col" else (j, me_c), device_id_type=MESH,
        )

    def f_send(j, source):
        return send_pieces(
            j, source, f_part.at[pl.ds(j * own_tiles, own_tiles)], f_recv, rsf_send, rsf_recv, "col")

    def b_send(d):
        j = at_chip(d, core)
        return pltpu.make_async_remote_copy(
            src_ref=b_part.at[pl.ds(j * own_tiles, own_tiles)], dst_ref=b_recv.at[y],
            send_sem=rsb_send.at[d], recv_sem=rsb_recv.at[y],
            device_id=(j, me_c), device_id_type=MESH,
        )

    def b_arrival(d):
        source = (y + d) & (chips - 1)
        return pltpu.make_async_remote_copy(
            src_ref=b_part.at[pl.ds(me_r * own_tiles, own_tiles)], dst_ref=b_recv.at[source],
            send_sem=rsb_send.at[d], recv_sem=rsb_recv.at[source],
            device_id=(at_chip(d, core), me_c), device_id_type=MESH,
        )

    def pair_copy(d):
        j = at_chip(d, 1 - core)
        return pltpu.make_async_remote_copy(
            src_ref=b_part.at[pl.ds(j * own_tiles, own_tiles)], dst_ref=pair.at[d],
            send_sem=pair_send.at[d], recv_sem=pair_recv.at[d],
            device_id=(sibling, me_c), device_id_type=MESH,
        )

    def df_send(j, source):
        return send_pieces(j, source, df_part.at[j], df_recv, dgf_send, dgf_recv, "col")

    def db_send(j, source):
        return send_pieces(j, source, db_part.at[j], db_recv, dgb_send, dgb_recv, "row")

    def d1_copy(j, source):
        return send_pieces(j, source, dots_row.at[me_r], dots_row, d1_send, d1_recv, "row")

    def d2_copy(j, source):
        return send_pieces(j, source, dots_col.at[me_c], dots_col, d2_send, d2_recv, "col")

    def start_gather():
        for t in range(own_tiles):
            piece = dir_ref[:, 128 * t : 128 * (t + 1)].astype(jnp.bfloat16)
            x_col[me_r * own_tiles + t] = piece
            x_row[me_c * own_tiles + t] = piece
        for d in far_first:
            gather_row(at_chip(d, core), me_r, at_chip(d, core)).start()
        gather_row(sibling, me_r, sibling).start()
        each_partner(n_col, me_c, lambda j: gather_col(j, me_c).start())

    def pass_row_on():
        for d in reversed(far_first):
            source = at_chip(d, core)
            gather_row(source, source, source).wait_recv()
            gather_row(sibling, source, at_chip(d, 1 - core)).start()
        gather_row(sibling, sibling, sibling).wait_recv()
        for d in reversed(far_first):
            source = at_chip(d, 1 - core)
            gather_row(sibling, source, source).wait_recv()

    def end_gather_sends():
        for d in far_first:
            gather_row(at_chip(d, core), me_r, at_chip(d, core)).wait_send()
            gather_row(sibling, at_chip(d, core), at_chip(d, 1 - core)).wait_send()
        gather_row(sibling, me_r, sibling).wait_send()
        all_cols.wait_send()

    def forward_tile(row, weigh):
        fields, weights = [], []
        for i in range(PER_ROW):
            code = row_table[0, row * PER_ROW + i]
            fields.append(weigh(x_col, code & 63, col_tiles))
            weights.append(tiles[code >> 6])
        return lax.dot_general(
            jnp.concatenate(fields, axis=1), jnp.concatenate(weights, axis=1),
            (((1,), (1,)), ((), ())), preferred_element_type=jnp.float32)

    def backward_tile(col, weigh):
        fields, weights = [], []
        for i in range(per_col):
            code = col_table[0, col * per_col + i]
            fields.append(weigh(x_row, code & 127, row_tiles))
            weights.append(tiles[code >> 7])
        return jnp.dot(
            jnp.concatenate(fields, axis=1), jnp.concatenate(weights, axis=0),
            preferred_element_type=jnp.float32)

    def field_of(x_ref, index, limit):
        return x_ref[index]

    def field_and_ones(x_ref, index, limit):
        unit = ones[jnp.where(index == limit, 1, 0)]
        return jnp.concatenate([x_ref[index], unit], axis=0)

    start_gather()
    live = count[0, 0]
    row_codes[...] = slot_table(rows[...], cols[...], live, PER_ROW, 6, col_tiles)
    col_codes[...] = slot_table(cols[...], rows[...], live, per_col, 7, row_tiles)
    table_copies = (
        pltpu.make_async_copy(row_codes, row_table, table_sem.at[0]),
        pltpu.make_async_copy(col_codes, col_table, table_sem.at[1]),
    )
    for copy in table_copies:
        copy.start()
    for i in range(tile_sem.shape[0]):
        tile_copy(i).wait()

    for copy in table_copies:
        copy.wait()

    def chunk_products(j, tile_of, part, first, d_part):
        for t in range(own_tiles):
            product = tile_of(j * own_tiles + t, field_and_ones if first else field_of)
            part[j * own_tiles + t] = product[:tasks].astype(part.dtype)
            if first:
                d_part[j, t : t + 1, :] = product[tasks : tasks + 1]
        if first:
            d_part[j, own_tiles:, :] = jnp.zeros((8 - own_tiles, 128), jnp.float32)

    def forward_products(first):
        def two(i, carry):
            for k in (2 * i, 2 * i + 1):
                chunk_products(partner(me_c, k, n_col), forward_tile, f_part, first, df_part)
            for k in (2 * i, 2 * i + 1):

                @pl.when(k != own_turn(n_col))
                def _(k=k):
                    j = partner(me_c, k, n_col)
                    f_send(j, me_c).start()
                    if first:
                        df_send(j, me_c).start()
            return carry

        lax.fori_loop(0, n_col // 2, two, 0)

    turns = far_first + [0]
    ahead = [(d, 0) for d in turns]
    behind = [(d, 1) for d in turns]
    order = [ahead[0]]
    for i in range(1, chips):
        order += [ahead[i], behind[i - 1]]
    order.append(behind[-1])

    def backward_products(first):
        def turn(k):
            d = pick(k, [d for d, final in order])
            final = pick(k, [final for d, final in order])
            return d, final, at_chip(d, core + (1 - final) * (1 - 2 * core))

        def two(i, carry):
            for k in (2 * i, 2 * i + 1):
                d, final, j = turn(k)
                chunk_products(j, backward_tile, b_part, first, db_part)
            for k in (2 * i, 2 * i + 1):
                d, final, j = turn(k)

                @pl.when(final == 0)
                def _(d=d):
                    pair_copy(d).start()

                @pl.when(final == 1)
                def _(d=d, j=j):
                    pair_copy(d).wait_recv()
                    for t in range(own_tiles):
                        b_part[j * own_tiles + t] = b_part[j * own_tiles + t] + pair[d, t]

                    @pl.when(d != 0)
                    def _():
                        b_send(d).start()

                if first:

                    @pl.when(j != me_r)
                    def _(j=j):
                        db_send(j, me_r).start()
            return carry

        lax.fori_loop(0, n_row // 2, two, 0)

    def gather_sums(n, own, send, recv, totals):
        def one(k, sums):
            j = (own + 1 + k) & (n - 1)
            send(j, j).wait_recv()
            return tuple(s + recv[j, t].astype(jnp.float32) for t, s in enumerate(sums))

        return lax.fori_loop(0, n - 1, one, totals)

    lane = lax.broadcasted_iota(jnp.int32, (tasks, 128), 1)
    task = lax.broadcasted_iota(jnp.int32, (tasks, 128), 0)

    def one_step(step, first):
        pass_row_on()
        forward_products(first)
        all_cols.wait_recv()
        backward_products(first)
        end_gather_sends()

        if first:
            df_recv[me_c] = df_part[me_c]
            db_recv[me_r] = db_part[me_r]
            all_df.wait_recv()
            all_db.wait_recv()
            total = sum(df_recv[i] for i in range(n_col)) + sum(db_recv[i] for i in range(n_row))
            degree[...] = 0.5 * total

        totals = tuple(
            f_part[me_c * own_tiles + t].astype(jnp.float32)
            + b_part[me_r * own_tiles + t].astype(jnp.float32)
            for t in range(own_tiles))
        totals = gather_sums(n_col, me_c, f_send, f_recv, totals)
        for d in reversed(far_first):
            b_arrival(d).wait_recv()
            source = (y + d) & (chips - 1)
            totals = tuple(s + b_recv[source, t] for t, s in enumerate(totals))

        pq = jnp.zeros((tasks, 128), jnp.float32)
        rq, qq, rr = pq, pq, pq
        images = []
        for t in range(own_tiles):
            part = slice(128 * t, 128 * (t + 1))
            p, r = dir_ref[:, part], res[:, part]
            q = p + coupling * (degree[t : t + 1, :] * p - 0.5 * totals[t])
            images.append(q)
            pq, rq, qq, rr = pq + p * q, rq + r * q, qq + q * q, rr + r * r
        row = jnp.zeros((tasks, 128), jnp.float32)
        for i, s in enumerate((pq, rq, qq, rr)):
            row = jnp.where(lane == task + tasks * i, jnp.sum(s, axis=1, keepdims=True), row)
        row = jnp.sum(row, axis=0, keepdims=True)
        dots_row[me_r] = row
        each_partner(n_row, me_r, lambda j: d1_copy(j, me_r).start())
        all_d1.wait_recv()
        dots_col[me_c] = sum(dots_row[i] for i in range(n_row))
        each_partner(n_col, me_c, lambda j: d2_copy(j, me_c).start())
        all_d2.wait_recv()
        sums = jnp.broadcast_to(sum(dots_col[i] for i in range(n_col)), (tasks, 128))
        pq, rq, qq, rr = (
            jnp.sum(jnp.where(lane == task + tasks * i, sums, 0.0), axis=1, keepdims=True)
            for i in range(4))
        size = rr / pq
        new = jnp.maximum(rr - 2.0 * size * rq + size * size * qq, 0.0)
        ratio = new / rr
        moves = []
        for t in range(own_tiles):
            part = slice(128 * t, 128 * (t + 1))
            p = dir_ref[:, part]
            r = res[:, part] - size * images[t]
            moves.append(size * p)
            res[:, part] = r
            dir_ref[:, part] = r + ratio * p

        @pl.when(step + 1 < ITERS)
        def _():
            start_gather()

        for t in range(own_tiles):
            part = slice(128 * t, 128 * (t + 1))
            sol[:, part] = sol[:, part] + moves[t]
        all_f.wait_send()
        for d in range(chips):
            pair_copy(d).wait_send()
        for d in far_first:
            b_send(d).wait_send()
        all_d1.wait_send()
        all_d2.wait_send()
        if first:
            all_df.wait_send()
            all_db.wait_send()

    one_step(0, True)

    def later_step(step, carry):
        one_step(step, False)
        return carry

    lax.fori_loop(1, ITERS, later_step, 0)


def per_device(n_row, n_col, scores, tile_values, tile_rows, tile_cols, tile_count):
    tiles = tile_values[0, 0]
    rows, cols = tile_rows[0], tile_cols[0]
    slots = tiles.shape[0]
    tasks, piece = scores.shape
    own_tiles = piece // 128
    row_tiles, col_tiles = own_tiles * n_col, own_tiles * n_row
    per_col = slots // col_tiles
    f32 = jnp.float32
    dma = pltpu.SemaphoreType.DMA
    vmem = pl.BlockSpec(memory_space=pltpu.VMEM)
    smem = pl.BlockSpec(memory_space=pltpu.SMEM)
    sol, res = pl.pallas_call(
        functools.partial(cg_kernel, n_row, n_col, per_col),
        out_shape=(
            jax.ShapeDtypeStruct((tasks, piece), f32),
            jax.ShapeDtypeStruct((tasks, piece), f32),
        ),
        in_specs=[smem, vmem, vmem, vmem, pl.BlockSpec(memory_space=pl.ANY)],
        out_specs=(vmem, vmem),
        scratch_shapes=[
            pltpu.VMEM((slots, 128, 128), jnp.bfloat16),
            pltpu.VMEM((col_tiles + 1, tasks, 128), jnp.bfloat16),
            pltpu.VMEM((row_tiles + 1, tasks, 128), jnp.bfloat16),
            pltpu.VMEM((row_tiles, tasks, 128), F_TYPE),
            pltpu.VMEM((col_tiles, tasks, 128), B_TYPE),
            pltpu.VMEM((n_col, own_tiles, tasks, 128), F_TYPE),
            pltpu.VMEM((n_row // 2, own_tiles, tasks, 128), B_TYPE),
            pltpu.VMEM((n_row // 2, own_tiles, tasks, 128), B_TYPE),
            pltpu.VMEM((n_col, 8, 128), f32),
            pltpu.VMEM((n_row, 8, 128), f32),
            pltpu.VMEM((n_col, 8, 128), f32),
            pltpu.VMEM((n_row, 8, 128), f32),
            pltpu.VMEM((2, 16, 128), jnp.bfloat16),
            pltpu.VMEM((tasks, piece), f32),
            pltpu.VMEM((8, 128), f32),
            pltpu.VMEM((n_row, 1, 128), f32),
            pltpu.VMEM((n_col, 1, 128), f32),
            pltpu.VMEM((1, slots), jnp.int32),
            pltpu.VMEM((1, slots), jnp.int32),
            pltpu.SMEM((1, slots), jnp.int32),
            pltpu.SMEM((1, slots), jnp.int32),
            dma((8,)), dma((2,)),
            dma((n_row,)), dma((n_row,)), dma((1,)), dma((1,)),
            dma((1,)), dma((n_col,)), dma((n_row // 2,)), dma((n_row // 2,)),
            dma((n_row // 2,)), dma((n_row // 2,)),
            dma((1,)), dma((1,)), dma((1,)), dma((1,)),
            dma((1,)), dma((1,)), dma((1,)), dma((1,)),
        ],
        compiler_params=pltpu.CompilerParams(
            collective_id=0, has_side_effects=True, vmem_limit_bytes=56 * 1024 * 1024
        ),
    )(tile_count, rows, cols, scores, tiles)
    return pl.pallas_call(
        copy_kernel,
        out_shape=(
            jax.ShapeDtypeStruct((tasks, piece), f32),
            jax.ShapeDtypeStruct((tasks, piece), f32),
        ),
        in_specs=[vmem, vmem],
        out_specs=(vmem, vmem),
    )(sol, res)


def solution(mesh):
    return jax.shard_map(
        functools.partial(per_device, mesh.shape["row"], mesh.shape["col"]),
        mesh=mesh,
        in_specs=(
            P(None, ("row", "col")),
            P("row", "col", None, None, None),
            P("row", "col", None),
            P("row", "col", None),
            P("row", "col"),
        ),
        out_specs=(P(None, ("row", "col")), P(None, ("row", "col"))),
        check_vma=False,
    )
```

time: 107 us -> 105 us (0.981)
  Pallas kernels: 105 us -> 103 us
    pallas_call x1, Pallas kernels: 104 us -> 102 us  [per_device(): pl.pallas_call(functools.partial(cg_kernel, n_row, n_col, per_col), out_s...]
where the time goes in v4:
time: 105 us
  Pallas kernels  103 us (98%)
  between operations  1.29 us (1%)
    pallas_call x1, Pallas kernels, per_device(): pl.pallas_call(functools.partial(cg_kernel, n_row, n_col, per_col), out_s...  102 us

profile of v4, /device:TPU:0, one launch (start us, length us, event | category | flops | bytes accessed | tf_op | source)
XLA Modules:
  0.0 104.7 jit_solution(14830801992317008714)
XLA Ops:
  1.3 101.7 %shard_map.68 = (f32[32,768]{1,0:T(8,128)}, f32[32,768]{1,0:T(8,128)}) custom-call(s32[1,1]{1,0:T(1,128)S(6)} %copy.7.count, s32[1,480]{1,0:T(1,128)} %bitcast.4, s32[1,480]{1,0:T(1,128)} %bitcast.5, f32[32,768]{1,0:T(8,128)} %scores.1, bf16[480,128,128]{2,1,0:T(8,128)(2,1)} %bitcast.3), custom_call_target="tpu_custom_call" | custom-call | tf_op jit(solution)/shard_map/pallas_call | solution.py:465
  103.0 1.6 %shard_map.69 = (f32[32,768]{1,0:T(8,128)}, f32[32,768]{1,0:T(8,128)}) custom-call(f32[32,768]{1,0:T(8,128)} %get-tuple-element.4.sol_in, f32[32,768]{1,0:T(8,128)} %get-tuple-element.5.res_in), custom_call_target="tpu_custom_call" | custom-call | tf_op jit(solution)/shard_map/pallas_call | solution.py:506

commit v5 on v4

--- a/solution.py
+++ b/solution.py
@@ -69,7 +69,7 @@
     df_part, db_part, df_recv, db_recv, ones, dir_ref, degree, dots_row, dots_col,
     row_codes, col_codes, row_table, col_table,
     tile_sem, table_sem,
-    agr_send, agr_recv, agc_send, agc_recv,
+    agr_send, agr_recv, agc_send, agc_recv, first_x, first_z,
     rsf_send, rsf_recv, rsb_send, rsb_recv, pair_send, pair_recv,
     dgf_send, dgf_recv, dgb_send, dgb_recv,
     d1_send, d1_recv, d2_send, d2_recv,
@@ -79,9 +79,16 @@
     y, core = me_r >> 1, me_r & 1
     chips = n_row // 2
     sibling = me_r + 1 - 2 * core
-    far_first = sorted(range(1, chips), key=lambda d: -min(d, chips - d))
+    side_x, side_z = spread(n_col)
+    x, z = me_c // side_z, me_c % side_z
+
+    def by_distance(side):
+        return sorted(range(1, side), key=lambda d: -min(d, side - d))
+
+    far_first, far_x, far_z = by_distance(chips), by_distance(side_x), by_distance(side_z)
     tasks = scores.shape[0]
     own_tiles = scores.shape[1] // 128
+    half = own_tiles // 2
     slots = tiles.shape[0]
     col_tiles = b_part.shape[0]
     row_tiles = f_part.shape[0]
@@ -148,7 +155,9 @@
         )
 
     others_row, others_col = n_row - 1, n_col - 1
-    all_cols = all_of(x_row, others_col * own_tiles, agc_send, agc_recv)
+    all_cols = all_of(x_row, others_col * own_tiles, agc_send, agc_send)
+    second = half * (side_x * (side_z - 1) + side_z * (side_x - 1))
+    second_phase = all_of(x_row, second, agc_recv, agc_recv)
     all_f = all_of(f_part, others_col * own_tiles, rsf_send, rsf_send)
     all_df = all_of(df_recv, others_col, dgf_send, dgf_recv)
     all_db = all_of(db_recv, others_row, dgb_send, dgb_recv)
@@ -158,13 +167,38 @@
     def at_chip(d, on_core):
         return ((y + d) & (chips - 1)) * 2 + on_core
 
-    def gather_col(j, source):
-        part = pl.ds(source * own_tiles, own_tiles)
+    def at_place(dx, dz):
+        return ((x + dx) & (side_x - 1)) * side_z + ((z + dz) & (side_z - 1))
+
+    def gather_half(target, source, which, recv_sem):
+        part = pl.ds(source * own_tiles + which * half, half)
         return pltpu.make_async_remote_copy(
             src_ref=x_row.at[part], dst_ref=x_row.at[part],
-            send_sem=agc_send.at[0], recv_sem=agc_recv.at[0],
-            device_id=(me_r, j), device_id_type=MESH,
-        )
+            send_sem=agc_send.at[0], recv_sem=recv_sem,
+            device_id=(me_r, target), device_id_type=MESH,
+        )
+
+    def start_cols():
+        for d in far_x:
+            gather_half(at_place(d, 0), me_c, 0, first_x.at[x]).start()
+        for d in far_z:
+            gather_half(at_place(0, d), me_c, 1, first_z.at[z]).start()
+        pass_x_on(0)
+        pass_z_on(0)
+
+    def pass_x_on(dx):
+        source = at_place(dx, 0)
+        if dx:
+            gather_half(source, source, 0, first_x.at[(x + dx) & (side_x - 1)]).wait_recv()
+        for d in far_z:
+            gather_half(at_place(0, d), source, 0, agc_recv.at[0]).start()
+
+    def pass_z_on(dz):
+        source = at_place(0, dz)
+        if dz:
+            gather_half(source, source, 1, first_z.at[(z + dz) & (side_z - 1)]).wait_recv()
+        for d in far_x:
+            gather_half(at_place(d, 0), source, 1, agc_recv.at[0]).start()
 
     def send_pieces(j, source, part, recv, send_sem, recv_sem, axis):
         return pltpu.make_async_remote_copy(
@@ -221,13 +255,23 @@
         for d in far_first:
             gather_row(at_chip(d, core), me_r, at_chip(d, core)).start()
         gather_row(sibling, me_r, sibling).start()
-        each_partner(n_col, me_c, lambda j: gather_col(j, me_c).start())
-
-    def pass_row_on():
-        for d in reversed(far_first):
-            source = at_chip(d, core)
-            gather_row(source, source, source).wait_recv()
-            gather_row(sibling, source, at_chip(d, 1 - core)).start()
+        start_cols()
+
+    def pass_y_on(d):
+        source = at_chip(d, core)
+        gather_row(source, source, source).wait_recv()
+        gather_row(sibling, source, at_chip(d, 1 - core)).start()
+
+    def pass_on():
+        for d in reversed(far_first[1:]):
+            pass_y_on(d)
+        for d in reversed(far_x[1:]):
+            pass_x_on(d)
+        for d in reversed(far_z[1:]):
+            pass_z_on(d)
+        pass_y_on(far_first[0])
+        pass_x_on(far_x[0])
+        pass_z_on(far_z[0])
         gather_row(sibling, sibling, sibling).wait_recv()
         for d in reversed(far_first):
             source = at_chip(d, 1 - core)
@@ -240,15 +284,32 @@
         gather_row(sibling, me_r, sibling).wait_send()
         all_cols.wait_send()
 
-    def forward_tile(row, weigh):
-        fields, weights = [], []
-        for i in range(PER_ROW):
-            code = row_table[0, row * PER_ROW + i]
-            fields.append(weigh(x_col, code & 63, col_tiles))
-            weights.append(tiles[code >> 6])
+    def wide_dot(fields, weights):
         return lax.dot_general(
-            jnp.concatenate(fields, axis=1), jnp.concatenate(weights, axis=1),
+            fields, jnp.concatenate(weights, axis=1),
             (((1,), (1,)), ((), ())), preferred_element_type=jnp.float32)
+
+    def forward_tiles(row, weigh):
+        sums, last_fields, last_weights = [], [], []
+        for r in (row, row + 1):
+            fields, weights = [], []
+            for i in range(PER_ROW):
+                code = row_table[0, r * PER_ROW + i]
+                fields.append(weigh(x_col, code & 63, col_tiles))
+                weights.append(tiles[code >> 6])
+            sums.append(wide_dot(jnp.concatenate(fields[:-1], axis=1), weights[:-1]))
+            last_fields.append(fields[-1])
+            last_weights.append(weights[-1])
+        zeros = jnp.zeros_like(last_fields[0])
+        lines = jnp.concatenate([
+            jnp.concatenate([last_fields[0], zeros], axis=1),
+            jnp.concatenate([zeros, last_fields[1]], axis=1)], axis=0)
+        last = wide_dot(lines, last_weights)
+        height = zeros.shape[0]
+        return [sums[0] + last[:height], sums[1] + last[height:]]
+
+    def backward_tiles(col, weigh):
+        return [backward_tile(col, weigh), backward_tile(col + 1, weigh)]
 
     def backward_tile(col, weigh):
         fields, weights = [], []
@@ -283,19 +344,20 @@
     for copy in table_copies:
         copy.wait()
 
-    def chunk_products(j, tile_of, part, first, d_part):
-        for t in range(own_tiles):
-            product = tile_of(j * own_tiles + t, field_and_ones if first else field_of)
-            part[j * own_tiles + t] = product[:tasks].astype(part.dtype)
-            if first:
-                d_part[j, t : t + 1, :] = product[tasks : tasks + 1]
+    def chunk_products(j, tiles_of, part, first, d_part):
+        for t in range(0, own_tiles, 2):
+            products = tiles_of(j * own_tiles + t, field_and_ones if first else field_of)
+            for i, product in enumerate(products):
+                part[j * own_tiles + t + i] = product[:tasks].astype(part.dtype)
+                if first:
+                    d_part[j, t + i : t + i + 1, :] = product[tasks : tasks + 1]
         if first:
             d_part[j, own_tiles:, :] = jnp.zeros((8 - own_tiles, 128), jnp.float32)
 
     def forward_products(first):
         def two(i, carry):
             for k in (2 * i, 2 * i + 1):
-                chunk_products(partner(me_c, k, n_col), forward_tile, f_part, first, df_part)
+                chunk_products(partner(me_c, k, n_col), forward_tiles, f_part, first, df_part)
             for k in (2 * i, 2 * i + 1):
 
                 @pl.when(k != own_turn(n_col))
@@ -311,10 +373,7 @@
     turns = far_first + [0]
     ahead = [(d, 0) for d in turns]
     behind = [(d, 1) for d in turns]
-    order = [ahead[0]]
-    for i in range(1, chips):
-        order += [ahead[i], behind[i - 1]]
-    order.append(behind[-1])
+    order = ahead[:-1] + behind[:-1] + [ahead[-1], behind[-1]]
 
     def backward_products(first):
         def turn(k):
@@ -325,7 +384,7 @@
         def two(i, carry):
             for k in (2 * i, 2 * i + 1):
                 d, final, j = turn(k)
-                chunk_products(j, backward_tile, b_part, first, db_part)
+                chunk_products(j, backward_tiles, b_part, first, db_part)
             for k in (2 * i, 2 * i + 1):
                 d, final, j = turn(k)
 
@@ -364,9 +423,9 @@
     task = lax.broadcasted_iota(jnp.int32, (tasks, 128), 0)
 
     def one_step(step, first):
-        pass_row_on()
+        pass_on()
         forward_products(first)
-        all_cols.wait_recv()
+        second_phase.wait_recv()
         backward_products(first)
         end_gather_sends()
 
@@ -494,6 +553,7 @@
             pltpu.SMEM((1, slots), jnp.int32),
             dma((8,)), dma((2,)),
             dma((n_row,)), dma((n_row,)), dma((1,)), dma((1,)),
+            dma((spread(n_col)[0],)), dma((spread(n_col)[1],)),
             dma((1,)), dma((n_col,)), dma((n_row // 2,)), dma((n_row // 2,)),
             dma((n_row // 2,)), dma((n_row // 2,)),
             dma((1,)), dma((1,)), dma((1,)), dma((1,)),

time: 105 us -> 101 us (0.962)
  Pallas kernels: 103 us -> 100 us
    pallas_call x1, Pallas kernels: 102 us -> 98.3 us  [per_device(): pl.pallas_call(functools.partial(cg_kernel, n_row, n_col, per_col), out_s...]
where the time goes in v5:
time: 101 us
  Pallas kernels  100 us (99%)
  between operations  1.29 us (1%)
    pallas_call x1, Pallas kernels, per_device(): pl.pallas_call(functools.partial(cg_kernel, n_row, n_col, per_col), out_s...  98.3 us

profile of v5, /device:TPU:0, one launch (start us, length us, event | category | flops | bytes accessed | tf_op | source)
XLA Modules:
  0.0 101.2 jit_solution(15465548453165761995)
XLA Ops:
  1.3 98.3 %shard_map.68 = (f32[32,768]{1,0:T(8,128)}, f32[32,768]{1,0:T(8,128)}) custom-call(s32[1,1]{1,0:T(1,128)S(6)} %copy.7.count, s32[1,480]{1,0:T(1,128)} %bitcast.4, s32[1,480]{1,0:T(1,128)} %bitcast.5, f32[32,768]{1,0:T(8,128)} %scores.1, bf16[480,128,128]{2,1,0:T(8,128)(2,1)} %bitcast.3), custom_call_target="tpu_custom_call" | custom-call | tf_op jit(solution)/shard_map/pallas_call | solution.py:524
  99.6 1.6 %shard_map.69 = (f32[32,768]{1,0:T(8,128)}, f32[32,768]{1,0:T(8,128)}) custom-call(f32[32,768]{1,0:T(8,128)} %get-tuple-element.4.sol_in, f32[32,768]{1,0:T(8,128)} %get-tuple-element.5.res_in), custom_call_target="tpu_custom_call" | custom-call | tf_op jit(solution)/shard_map/pallas_call | solution.py:566

commit v6 on v5

--- a/solution.py
+++ b/solution.py
@@ -355,10 +355,11 @@
             d_part[j, own_tiles:, :] = jnp.zeros((8 - own_tiles, 128), jnp.float32)
 
     def forward_products(first):
-        def two(i, carry):
-            for k in (2 * i, 2 * i + 1):
+        def four(i, carry):
+            turn = [4 * i + n for n in range(4)]
+            for k in turn:
                 chunk_products(partner(me_c, k, n_col), forward_tiles, f_part, first, df_part)
-            for k in (2 * i, 2 * i + 1):
+            for k in turn:
 
                 @pl.when(k != own_turn(n_col))
                 def _(k=k):
@@ -368,7 +369,7 @@
                         df_send(j, me_c).start()
             return carry
 
-        lax.fori_loop(0, n_col // 2, two, 0)
+        lax.fori_loop(0, n_col // 4, four, 0)
 
     turns = far_first + [0]
     ahead = [(d, 0) for d in turns]
@@ -461,10 +462,14 @@
             row = jnp.where(lane == task + tasks * i, jnp.sum(s, axis=1, keepdims=True), row)
         row = jnp.sum(row, axis=0, keepdims=True)
         dots_row[me_r] = row
-        each_partner(n_row, me_r, lambda j: d1_copy(j, me_r).start())
+        for k in range(n_row):
+            if k != own_turn(n_row):
+                d1_copy(partner(me_r, k, n_row), me_r).start()
         all_d1.wait_recv()
         dots_col[me_c] = sum(dots_row[i] for i in range(n_row))
-        each_partner(n_col, me_c, lambda j: d2_copy(j, me_c).start())
+        for k in range(n_col):
+            if k != own_turn(n_col):
+                d2_copy(partner(me_c, k, n_col), me_c).start()
         all_d2.wait_recv()
         sums = jnp.broadcast_to(sum(dots_col[i] for i in range(n_col)), (tasks, 128))
         pq, rq, qq, rr = (

time: 101 us -> 99.1 us (0.981)
  Pallas kernels: 100 us -> 97.7 us
    pallas_call x1, Pallas kernels: 98.3 us -> 96 us  [per_device(): pl.pallas_call(functools.partial(cg_kernel, n_row, n_col, per_col), out_s...]
where the time goes in v6:
time: 99.1 us; the launch traced here: 98.9 us
  Pallas kernels  97.7 us (99%)
  between operations  1.29 us (1%)
    pallas_call x1, Pallas kernels, per_device(): pl.pallas_call(functools.partial(cg_kernel, n_row, n_col, per_col), out_s...  96 us

profile of v6, /device:TPU:0, one launch (start us, length us, event | category | flops | bytes accessed | tf_op | source)
XLA Modules:
  0.0 98.9 jit_solution(10490363704536079957)
XLA Ops:
  1.3 96.0 %shard_map.68 = (f32[32,768]{1,0:T(8,128)}, f32[32,768]{1,0:T(8,128)}) custom-call(s32[1,1]{1,0:T(1,128)S(6)} %copy.7.count, s32[1,480]{1,0:T(1,128)} %bitcast.4, s32[1,480]{1,0:T(1,128)} %bitcast.5, f32[32,768]{1,0:T(8,128)} %scores.1, bf16[480,128,128]{2,1,0:T(8,128)(2,1)} %bitcast.3), custom_call_target="tpu_custom_call" | custom-call | tf_op jit(solution)/shard_map/pallas_call | solution.py:529
  97.3 1.6 %shard_map.69 = (f32[32,768]{1,0:T(8,128)}, f32[32,768]{1,0:T(8,128)}) custom-call(f32[32,768]{1,0:T(8,128)} %get-tuple-element.4.sol_in, f32[32,768]{1,0:T(8,128)} %get-tuple-element.5.res_in), custom_call_target="tpu_custom_call" | custom-call | tf_op jit(solution)/shard_map/pallas_call | solution.py:571

commit v7 on v6

--- a/solution.py
+++ b/solution.py
@@ -528,10 +528,7 @@
     smem = pl.BlockSpec(memory_space=pltpu.SMEM)
     sol, res = pl.pallas_call(
         functools.partial(cg_kernel, n_row, n_col, per_col),
-        out_shape=(
-            jax.ShapeDtypeStruct((tasks, piece), f32),
-            jax.ShapeDtypeStruct((tasks, piece), f32),
-        ),
+        out_shape=(pltpu.VMEM((tasks, piece), f32), pltpu.VMEM((tasks, piece), f32)),
         in_specs=[smem, vmem, vmem, vmem, pl.BlockSpec(memory_space=pl.ANY)],
         out_specs=(vmem, vmem),
         scratch_shapes=[
@@ -576,7 +573,10 @@
         ),
         in_specs=[vmem, vmem],
         out_specs=(vmem, vmem),
-    )(sol, res)
+    )(
+        pltpu.with_memory_space_constraint(sol, pltpu.VMEM),
+        pltpu.with_memory_space_constraint(res, pltpu.VMEM),
+    )
 
 
 def solution(mesh):

time: 99.1 us -> 97.5 us (0.984)
  Pallas kernels: 97.7 us -> 96.1 us
where the time goes in v7:
time: 97.5 us; the launch traced here: 97.3 us
  Pallas kernels  96.1 us (99%)
  between operations  1.29 us (1%)
    pallas_call x1, Pallas kernels, per_device(): pl.pallas_call(functools.partial(cg_kernel, n_row, n_col, per_col), out_s...  95.4 us

profile of v7, /device:TPU:0, one launch (start us, length us, event | category | flops | bytes accessed | tf_op | source)
XLA Modules:
  0.0 97.3 jit_solution(14052358386211244306)
XLA Ops:
  1.3 95.4 %shard_map.68 = (f32[32,768]{1,0:T(8,128)S(1)}, f32[32,768]{1,0:T(8,128)S(1)}) custom-call(s32[1,1]{1,0:T(1,128)S(6)} %copy.7.count, s32[1,480]{1,0:T(1,128)} %bitcast.4, s32[1,480]{1,0:T(1,128)} %bitcast.5, f32[32,768]{1,0:T(8,128)} %scores.1, bf16[480,128,128]{2,1,0:T(8,128)(2,1)} %bitcast.3), custom_call_target="tpu_custom_call" | custom-call | tf_op jit(solution)/shard_map/pallas_call | solution.py:529
  96.7 0.7 shard_map.69

commit v8 on v7

--- a/solution.py
+++ b/solution.py
@@ -248,13 +248,15 @@
         return send_pieces(j, source, dots_col.at[me_c], dots_col, d2_send, d2_recv, "col")
 
     def start_gather():
+        pieces = [
+            dir_ref[:, 128 * t : 128 * (t + 1)].astype(jnp.bfloat16) for t in range(own_tiles)]
         for t in range(own_tiles):
-            piece = dir_ref[:, 128 * t : 128 * (t + 1)].astype(jnp.bfloat16)
-            x_col[me_r * own_tiles + t] = piece
-            x_row[me_c * own_tiles + t] = piece
+            x_col[me_r * own_tiles + t] = pieces[t]
         for d in far_first:
             gather_row(at_chip(d, core), me_r, at_chip(d, core)).start()
         gather_row(sibling, me_r, sibling).start()
+        for t in range(own_tiles):
+            x_row[me_c * own_tiles + t] = pieces[t]
         start_cols()
 
     def pass_y_on(d):

time: 97.5 us -> 97.5 us (level)
  no operation moved by 1% of the time
where the time goes in v8:
time: 97.5 us; the launch traced here: 97.3 us
  Pallas kernels  96 us (98%)
  between operations  1.29 us (1%)
    pallas_call x1, Pallas kernels, per_device(): pl.pallas_call(functools.partial(cg_kernel, n_row, n_col, per_col), out_s...  95.3 us

profile of v8, /device:TPU:0, one launch (start us, length us, event | category | flops | bytes accessed | tf_op | source)
XLA Modules:
  0.0 97.3 jit_solution(8882280762737697222)
XLA Ops:
  1.3 95.3 %shard_map.68 = (f32[32,768]{1,0:T(8,128)S(1)}, f32[32,768]{1,0:T(8,128)S(1)}) custom-call(s32[1,1]{1,0:T(1,128)S(6)} %copy.7.count, s32[1,480]{1,0:T(1,128)} %bitcast.4, s32[1,480]{1,0:T(1,128)} %bitcast.5, f32[32,768]{1,0:T(8,128)} %scores.1, bf16[480,128,128]{2,1,0:T(8,128)(2,1)} %bitcast.3), custom_call_target="tpu_custom_call" | custom-call | tf_op jit(solution)/shard_map/pallas_call | solution.py:531
  96.6 0.7 shard_map.69
